TPU v7x, 32 devices: a whole 2x2x4 slice. The times are simulated.
32 devices in a mesh: batch: 8 (over z, core), seq: 4 (over y, x).
Axes of the slice: x: 2, y: 2, z: 4, core: 2. Of those that a mesh axis runs over, the one named last changes fastest.
Arguments:
- tokens: bfloat16 [8, 1024, 768], P('batch', 'seq'), may hold values from -6 to 6
- cotangent: bfloat16 [8, 1024, 768], P('batch', 'seq'), may hold values from -6 to 6
- w_query: bfloat16 [768, 768], replicated, may hold values from -0.21875 to 0.21875
- b_query: float32 [768], replicated, may hold values from -5 to 5
- w_key: bfloat16 [768, 768], replicated, may hold values from -0.21875 to 0.21875
- w_value: bfloat16 [768, 768], replicated, may hold values from -0.21875 to 0.21875
- b_value: float32 [768], replicated, may hold values from -3 to 3
- w_out: bfloat16 [768, 768], replicated, may hold values from -1.75 to 1.75
- b_out: float32 [768], replicated, may hold values from -3 to 3
- first_gain: float32 [768], replicated, may hold values from 0.1 to 1.9
- first_shift: float32 [768], replicated, may hold values from -3 to 3
- w_inner: bfloat16 [768, 3072], replicated, may hold values from -0.21875 to 0.21875
- b_inner: float32 [3072], replicated, may hold values from -3 to 3
- w_outer: bfloat16 [3072, 768], replicated, may hold values from -0.109375 to 0.109375
- b_outer: float32 [768], replicated, may hold values from -3 to 3
- second_gain: float32 [768], replicated, may hold values from 0.1 to 1.9
- second_shift: float32 [768], replicated, may hold values from -3 to 3
- global_counts: int32 [8], P('batch'), may hold values from 2 to 4
- random_blocks: int32 [8, 16, 12, 3], P('batch', 'seq'), may hold values from 0 to 15, as said below
Outputs:
- layer_out: bfloat16 [8, 1024, 768], P('batch', 'seq')
- token_grad: float32 [8, 1024, 768], P('batch', 'seq')
- grad_w_query: float32 [768, 768], replicated
- grad_b_query: float32 [768], replicated
- grad_w_key: float32 [768, 768], replicated
- grad_w_value: float32 [768, 768], replicated
- grad_b_value: float32 [768], replicated
- grad_w_out: float32 [768, 768], replicated
- grad_b_out: float32 [768], replicated
- grad_first_gain: float32 [768], replicated
- grad_first_shift: float32 [768], replicated
- grad_w_inner: float32 [768, 3072], replicated
- grad_b_inner: float32 [3072], replicated
- grad_w_outer: float32 [3072, 768], replicated
- grad_b_outer: float32 [768], replicated
- grad_second_gain: float32 [768], replicated
- grad_second_shift: float32 [768], replicated
Inputs may be any that keep to these rules, and one draw needn't show every extreme that they name: `random_blocks`: in each sequence, the 144 entries of the query blocks 4 * i to 4 * i + 3 name blocks of each range 4 * j to 4 * j + 3 exactly 36 times.
All inputs are finite; a program needn't handle non-finite values.
Results may differ from a plain program's by a relative error of at most 0.015.
Values may be sent and summed in bfloat16 or wider, within the bound.
No kernel may reach another device: no remote copies, remote signals or barrier semaphores. Data moves between devices by JAX's collectives and lax.ppermute only.
A program may use at most 384 MiB of HBM per device.

v0:
```python
import functools
import math

import jax
import jax.numpy as jnp
from jax import lax
from jax.experimental import pallas as pl
from jax.experimental.pallas import tpu as pltpu
from jax.sharding import PartitionSpec as P

HEADS = 12
HD = 64
BLK = 64
GMAX = 4
QUAD = 4
EPSILON = 1e-06
NEGATIVE = -1e30
BF = jnp.bfloat16
F32 = jnp.float32
VMEM_BYTES = 24 * 1024 * 1024
EVENT_FLOPS = 50 * 10**6

NN = (((1,), (0,)), ((), ()))
NT = (((1,), (1,)), ((), ()))
TN = (((0,), (0,)), ((), ()))


def mm(a, b, dims=NN):
    return lax.dot_general(a, b, dims, preferred_element_type=F32)


def params(**kw):
    return pltpu.CompilerParams(vmem_limit_bytes=VMEM_BYTES, **kw)


def cost(flops, bytes_accessed, exps=0):
    return pl.CostEstimate(flops=flops * 100, bytes_accessed=bytes_accessed * 100, transcendentals=exps * 100)


def ordered(body, order, in_specs, args, name, out_specs, out_shape, **kw):
    if order is None:
        return pl.pallas_call(
            body, in_specs=in_specs, out_specs=out_specs, out_shape=out_shape, name=name, **kw
        )(*args)
    one = not isinstance(out_shape, (list, tuple))
    specs, shapes = ([out_specs], [out_shape]) if one else (list(out_specs), list(out_shape))
    marks = [] if order.last is None else [order.last]
    n, made = len(args), len(shapes)
    mark = jax.ShapeDtypeStruct((8, 128), F32)

    def kernel(*refs):
        outs = refs[n + len(marks) :]
        outs[made][...] = jnp.zeros_like(outs[made])
        body(*refs[:n], *outs[:made], *outs[made + 1 :])

    mark_spec = pl.BlockSpec((8, 128), lambda *_: (0, 0))
    *out, order.last = pl.pallas_call(
        kernel,
        in_specs=list(in_specs) + [pl.BlockSpec(memory_space=pl.ANY)] * len(marks),
        out_specs=specs + [mark_spec],
        out_shape=shapes + [mark],
        name=name,
        **kw,
    )(*args, *marks)
    return out[0] if one else out


def whole(shape):
    return pl.BlockSpec(shape, lambda *_: (0,) * len(shape))


def half_mask(values, side):
    lane = lax.broadcasted_iota(jnp.int32, values.shape, 1)
    keep = lane < HD if side == 0 else lane >= HD
    return jnp.where(keep, values, jnp.zeros_like(values))


def attend_body(rows, *refs):
    n = len(rows)
    pieces = refs[:n]
    wq, wk, wv, vec, bias = refs[n : n + 5]
    q_out, k_out, v_out, o_out, lse_out = refs[n + 5 : n + 10]
    vt, sc, ot = refs[n + 10 :]
    q = (mm(pieces[0][...], wq[...]) + vec[0:1, :]).astype(BF)
    q_out[...] = (q.astype(F32) * (1.0 / math.sqrt(HD))).astype(BF)
    start = 0
    for piece, count in zip(pieces, rows):
        x = piece[...]
        k_out[0, start : start + count, :] = mm(x, wk[...]).astype(BF)
        v = mm(x, wv[...]) + vec[1:2, :]
        v_out[0, start : start + count, :] = v.astype(BF)
        vt[:, start : start + count] = v.T.astype(BF)
        start += count
    total = start
    step = 256
    per = step // BLK
    for head in range(QUAD):
        lanes = slice(head // 2 * 128, head // 2 * 128 + 128)
        qh = half_mask(q_out[:, lanes], head % 2)
        top = jnp.full((1, qh.shape[0]), NEGATIVE, F32)
        for c in range(total // step):
            part = mm(k_out[0, c * step : (c + 1) * step, lanes], qh, NT)
            for b in range(per):
                row = bias[head, c * per + b : c * per + b + 1, :]
                s = part[b * BLK : (b + 1) * BLK, :] + row
                sc[c * step + b * BLK : c * step + (b + 1) * BLK, :] = s
                top = jnp.maximum(top, jnp.max(s, axis=0, keepdims=True))
        acc = jnp.zeros((HD, qh.shape[0]), F32)
        norm = jnp.zeros((1, qh.shape[0]), F32)
        for c in range(total // step):
            e = jnp.exp(sc[c * step : (c + 1) * step, :] - top)
            norm = norm + jnp.sum(e, axis=0, keepdims=True)
            acc = acc + mm(vt[head * HD : (head + 1) * HD, c * step : (c + 1) * step], e.astype(BF))
        ot[head * HD : (head + 1) * HD, :] = acc / norm
        lse_out[0, head : head + 1, :] = top + jnp.log(norm)
    o_out[...] = ot[...].T


def attend(order, pieces, wq, wk, wv, vec, bias):
    rows = tuple(p.shape[0] for p in pieces)
    total = sum(rows)
    tok, width = pieces[0].shape
    groups = HEADS // QUAD
    cols = QUAD * HD
    col = lambda r: pl.BlockSpec((r, cols), lambda g: (0, g))
    return ordered(
        functools.partial(attend_body, rows),
        order,
        [whole((r, width)) for r in rows]
        + [col(width), col(width), col(width), col(vec.shape[0])]
        + [pl.BlockSpec((QUAD,) + bias.shape[1:], lambda g: (g, 0, 0))],
        (*pieces, *(pltpu.with_memory_space_constraint(w, pltpu.HBM) for w in (wq, wk, wv)), vec, bias),
        "attend",
        grid=(groups,),
        out_specs=[
            col(tok),
            pl.BlockSpec((1, total, cols), lambda g: (g, 0, 0)),
            pl.BlockSpec((1, total, cols), lambda g: (g, 0, 0)),
            col(tok),
            pl.BlockSpec((1, QUAD, tok), lambda g: (g, 0, 0)),
        ],
        out_shape=[
            pltpu.HBM((tok, width), BF),
            pltpu.HBM((groups, total, cols), BF),
            pltpu.HBM((groups, total, cols), BF),
            jax.ShapeDtypeStruct((tok, width), F32),
            jax.ShapeDtypeStruct((groups, QUAD, tok), F32),
        ],
        scratch_shapes=[
            pltpu.VMEM((cols, total), BF),
            pltpu.VMEM((total, tok), F32),
            pltpu.VMEM((cols, tok), F32),
        ],
        cost_estimate=cost(2 * total * 256 * (2 * HEADS * tok + 3 * width * 2), 4 * total * width * 2, HEADS * tok * total),
        compiler_params=params(),
    )


def norm_stats(values):
    mean = jnp.mean(values, axis=-1, keepdims=True)
    centred = values - mean
    r = lax.rsqrt(jnp.mean(centred * centred, axis=-1, keepdims=True) + EPSILON)
    return centred * r, r


def norm_back(e, u, r):
    return r * (e - jnp.mean(e, axis=-1, keepdims=True) - u * jnp.mean(e * u, axis=-1, keepdims=True))


def colsum(values):
    return jnp.sum(values, axis=0, keepdims=True)


def put_pieces(dst, base, block, mix, size=96):
    for p in range(block.shape[0] // size):
        at = pl.multiple_of(base + (p ^ mix) * size, 16)
        dst[pl.ds(at, size), :] = block[p * size : (p + 1) * size, :]


def feed_body(
    info, o_in, x_in, cot_in, wo_any, wi_any, wu_any, vec,
    layer_out, u1_out, r1_out, g_second_out, g_outer_out, slope, small_out, hid_t, send,
    wo, wi, wu, sems,
):
    copies = [
        pltpu.make_async_copy(src, dst, sems.at[i])
        for i, (src, dst) in enumerate(((wo_any, wo), (wi_any, wi), (wu_any, wu)))
    ]
    for c in copies:
        c.start()
    small_out[...] = jnp.zeros_like(small_out)
    width = wo.shape[0]
    chunks = wi.shape[1] // width
    b_out, fg, fs, b_outer, sg, ss = (vec[i : i + 1, :] for i in range(2, 8))
    att = o_in[...].astype(BF)
    copies[0].wait()
    first_in = x_in[...].astype(F32) + (mm(att, wo[...]) + b_out)
    u1, r1 = norm_stats(first_in)
    u1_out[...] = u1
    r1_out[...] = jnp.broadcast_to(r1, r1_out.shape)
    first = u1 * fg + fs
    low = first.astype(BF)
    copies[1].wait()
    copies[2].wait()
    out = jnp.zeros_like(first)
    for j in range(chunks):
        cols = slice(j * width, (j + 1) * width)
        v = mm(low, wi[:, cols]) + vec[8 + j : 9 + j, :]
        t = jnp.tanh(0.7978845608028654 * (v + 0.044715 * v * v * v))
        h = 0.5 * v * (1.0 + t)
        slope[:, cols] = 0.5 * (1.0 + t) + 0.5 * v * (1.0 - t * t) * (
            0.7978845608028654 * (1.0 + 3.0 * 0.044715 * v * v)
        )
        out = out + mm(h.astype(BF), wu[cols, :])
        put_pieces(hid_t, j * width, h.T.astype(BF), info[2 + 2 * j // chunks])
    u2, r2 = norm_stats(first + (out + b_outer))
    layer_out[...] = (u2 * sg + ss).astype(BF)
    cot = cot_in[...].astype(F32)
    small_out[4:5, :] = colsum(cot * u2)
    small_out[5:6, :] = colsum(cot)
    g_second = norm_back(cot * sg, u2, r2)
    g_second_out[...] = g_second
    g_outer = g_second.astype(BF)
    g_outer_out[...] = g_outer
    small_out[3:4, :] = colsum(g_outer.astype(F32))
    for j in range(chunks // 2):
        at = pl.multiple_of((j ^ info[1]) * width, width)
        send[j * width : (j + 1) * width, :] = mm(hid_t[pl.ds(at, width), :], g_outer).astype(BF)


VM = pl.BlockSpec(memory_space=pltpu.VMEM)
SM = pl.BlockSpec(memory_space=pltpu.SMEM)
ANYWHERE = pl.BlockSpec(memory_space=pl.ANY)


def feed(order, info, o, x, cot, wo, wi, wu, vec):
    tok, width = x.shape
    ff = wi.shape[1]
    return ordered(
        feed_body,
        order,
        [SM, VM, VM, VM, ANYWHERE, ANYWHERE, ANYWHERE, VM],
        (info, o, x, cot, wo, wi, wu, vec,),
        "feed",
        out_specs=[VM] * 9,
        out_shape=[
            jax.ShapeDtypeStruct((tok, width), BF),
            jax.ShapeDtypeStruct((tok, width), F32),
            jax.ShapeDtypeStruct((tok, 128), F32),
            jax.ShapeDtypeStruct((tok, width), F32),
            jax.ShapeDtypeStruct((tok, width), BF),
            jax.ShapeDtypeStruct((tok, ff), F32),
            jax.ShapeDtypeStruct((8, width), F32),
            jax.ShapeDtypeStruct((ff, tok), BF),
            pltpu.HBM((ff // 2, width), BF),
        ],
        scratch_shapes=[
            pltpu.VMEM((width, width), BF),
            pltpu.VMEM((width, ff), BF),
            pltpu.VMEM((ff, width), BF),
            pltpu.SemaphoreType.DMA((3,)),
        ],
        cost_estimate=cost(2 * tok * width * (5 * ff // 2 + width), 4 * (width * ff * 2), tok * ff),
        compiler_params=params(),
    )


def inner_back_body(
    info, u1_in, g_second_in, g_outer_in, slope, hid_t, wi_any, wu_any, vec,
    keep, g_in, low_t, back_out, small_out, send,
    wi, wu, sems,
):
    copies = [
        pltpu.make_async_copy(src, dst, sems.at[i]) for i, (src, dst) in enumerate(((wu_any, wu), (wi_any, wi)))
    ]
    for c in copies:
        c.start()
    small_out[...] = jnp.zeros_like(small_out)
    width = wi.shape[0]
    chunks = wi.shape[1] // width
    g_outer = g_outer_in[...]
    for j in range(chunks // 2):
        at = pl.multiple_of((j ^ info[0]) * width, width)
        keep[j * width : (j + 1) * width, :] = mm(hid_t[pl.ds(at, width), :], g_outer).astype(BF)
    flat_t = (u1_in[...] * vec[3:4, :] + vec[4:5, :]).T.astype(BF)
    for c in range(2):
        put_pieces(low_t.at[c], 0, flat_t, info[2 + c])
    back = g_second_in[...]
    copies[0].wait()
    copies[1].wait()
    for j in range(chunks):
        cols = slice(j * width, (j + 1) * width)
        gi = (mm(g_outer, wu[cols, :], NT) * slope[:, cols]).astype(BF)
        g_in[:, cols] = gi
        small_out[j : j + 1, :] = colsum(gi.astype(F32))
        back = back + mm(gi, wi[:, cols], NT)
    back_out[...] = back
    for j in range(chunks // 2):
        at = pl.multiple_of((j ^ info[1]) * width, width)
        send[j * width : (j + 1) * width, :] = mm(low_t[1 - info[4]], g_in[:, pl.ds(at, width)]).astype(BF)


def inner_back(order, info, u1, g_second, g_outer, slope, hid_t, wi, wu, vec):
    tok, width = u1.shape
    ff = wi.shape[1]
    half = pltpu.HBM((ff // 2, width), BF)
    return ordered(
        inner_back_body,
        order,
        [SM] + [VM] * 5 + [ANYWHERE] * 2 + [VM],
        (info, u1, g_second, g_outer, slope, hid_t, wi, wu, vec,),
        "inner_back",
        out_specs=[VM] * 6,
        out_shape=[
            half,
            jax.ShapeDtypeStruct((tok, ff), BF),
            jax.ShapeDtypeStruct((2, width, tok), BF),
            jax.ShapeDtypeStruct((tok, width), F32),
            jax.ShapeDtypeStruct((8, width), F32),
            half,
        ],
        scratch_shapes=[
            pltpu.VMEM((width, ff), BF),
            pltpu.VMEM((ff, width), BF),
            pltpu.SemaphoreType.DMA((2,)),
        ],
        cost_estimate=cost(2 * tok * width * 3 * ff, 4 * (width * ff * 2)),
        compiler_params=params(),
    )


def branch_back_body(
    info, o_in, u1_in, r1_in, back_in, g_in, low_t, wo_in, vec,
    keep, g_sum_out, g_att_out, dots_out, small_out, wo_a,
    att_t,
):
    small_out[...] = jnp.zeros_like(small_out)
    width = wo_in.shape[0]
    for j in range(keep.shape[0] // width):
        at = pl.multiple_of((j ^ info[0]) * width, width)
        keep[j * width : (j + 1) * width, :] = mm(low_t[info[4]], g_in[:, pl.ds(at, width)]).astype(BF)
    back, u1 = back_in[...], u1_in[...]
    small_out[1:2, :] = colsum(back * u1)
    small_out[2:3, :] = colsum(back)
    g_sum = norm_back(back * vec[3:4, :], u1, r1_in[:, 0:1])
    g_sum_out[...] = g_sum
    g_branch = g_sum.astype(BF)
    small_out[0:1, :] = colsum(g_branch.astype(F32))
    o = o_in[...]
    g_att = mm(g_branch, wo_in[...], NT).astype(BF)
    g_att_out[...] = g_att
    put_pieces(att_t, 0, o.T.astype(BF), info[2])
    wo_a[...] = mm(att_t[...], g_branch).astype(BF)
    head = lax.broadcasted_iota(jnp.int32, (16, width), 0)
    lane = lax.broadcasted_iota(jnp.int32, (16, width), 1)
    pick = jnp.where(lane // HD == head, 1.0, 0.0).astype(F32)
    dots_out[...] = lax.dot_general(
        pick, g_att.astype(F32) * o, NT, precision=lax.Precision.HIGHEST, preferred_element_type=F32
    )


def branch_back(order, info, o, u1, r1, back, g_in, low_t, wo, vec):
    tok, width = o.shape
    ff = g_in.shape[1]
    return ordered(
        branch_back_body,
        order,
        [SM] + [VM] * 8,
        (info, o, u1, r1, back, g_in, low_t, wo, vec,),
        "branch_back",
        out_specs=[VM] * 6,
        out_shape=[
            pltpu.HBM((ff // 2, width), BF),
            pltpu.HBM((tok, width), F32),
            pltpu.HBM((tok, width), BF),
            jax.ShapeDtypeStruct((16, tok), F32),
            jax.ShapeDtypeStruct((8, width), F32),
            pltpu.HBM((width, width), BF),
        ],
        scratch_shapes=[pltpu.VMEM((width, tok), BF)],
        cost_estimate=cost(2 * tok * width * (ff // 2 + 2 * width), 4 * width * ff),
        compiler_params=params(),
    )


def attend_back_body(q_in, k_in, v_in, g_in, bias, lse, dots, dq_out, dk_out, dv_out, kt, dqt):
    total = k_in.shape[1]
    step = 256
    per = step // BLK
    kt[...] = k_in[0].astype(F32).T.astype(BF)
    for pair in range(QUAD // 2):
        lanes = slice(pair * 128, pair * 128 + 128)
        qs = [half_mask(q_in[:, lanes], s) for s in range(2)]
        gs = [half_mask(g_in[:, lanes], s) for s in range(2)]
        dqs = [jnp.zeros((HD, q_in.shape[0]), F32) for _ in range(2)]
        for c in range(total // step):
            rows = slice(c * step, (c + 1) * step)
            kc = k_in[0, rows, lanes]
            vc = v_in[0, rows, lanes]
            dk = jnp.zeros((step, 128), F32)
            dv = jnp.zeros((step, 128), F32)
            for s in range(2):
                head = pair * 2 + s
                sc = mm(kc, qs[s], NT)
                dp = mm(vc, gs[s], NT)
                shift = bias[head, c * per : (c + 1) * per, :] - lse[0, head : head + 1, :]
                p = jnp.concatenate(
                    [jnp.exp(sc[b * BLK : (b + 1) * BLK, :] + shift[b : b + 1, :]) for b in range(per)], axis=0
                )
                ds = (p * (dp - dots[0, head : head + 1, :])).astype(BF)
                dv = dv + mm(p.astype(BF), gs[s])
                dk = dk + mm(ds, qs[s])
                dqs[s] = dqs[s] + mm(kt[head * HD : (head + 1) * HD, rows], ds)
            dk_out[0, rows, lanes] = dk.astype(BF)
            dv_out[0, rows, lanes] = dv.astype(BF)
        for s in range(2):
            head = pair * 2 + s
            dqt[head * HD : (head + 1) * HD, :] = dqs[s]
    dq_out[0] = (dqt[...].T * (1.0 / math.sqrt(HD))).astype(BF)


def attend_back(order, q, k, v, g, bias, lse, dots):
    tok, width = q.shape
    groups, total, cols = k.shape
    col = pl.BlockSpec((tok, cols), lambda i: (0, i))
    group = lambda r: pl.BlockSpec((1, r, cols), lambda i: (i, 0, 0))
    stat = pl.BlockSpec((1, QUAD, tok), lambda i: (i, 0, 0))
    return ordered(
        attend_back_body,
        order,
        [col, group(total), group(total), col]
        + [pl.BlockSpec((QUAD,) + bias.shape[1:], lambda i: (i, 0, 0)), stat, stat],
        (*(pltpu.with_memory_space_constraint(a, pltpu.HBM) for a in (q, k, v, g)), bias, lse, dots),
        "attend_back",
        grid=(groups,),
        out_specs=[group(tok), group(total), group(total)],
        out_shape=[jax.ShapeDtypeStruct((groups, r, cols), BF) for r in (tok, total, total)],
        scratch_shapes=[pltpu.VMEM((cols, total), BF), pltpu.VMEM((cols, tok), F32)],
        cost_estimate=cost(HEADS * 5 * 2 * tok * total * 256, 4 * total * width * 2, HEADS * tok * total),
        compiler_params=params(),
    )


def weights_body(rows, smalls, info, wo_grad, *refs):
    n = len(rows)
    small_in, refs = refs[:smalls], refs[smalls:]
    groups = HEADS // QUAD
    dqs, dks, dvs = refs[:3]
    pieces = refs[3 : 3 + n]
    keep, send = refs[3 + n : 5 + n]
    x0, x1, tmp, small = refs[5 + n :]
    own = rows[0]
    start = 0
    for piece, count in zip(pieces, rows):
        t = piece[...].astype(F32).T.astype(BF)
        for p in range(t.shape[0] // 96):
            for xt, mix in ((x0, info[2]), (x1, info[3])):
                if start < own or xt is x1:
                    at = pl.multiple_of((p ^ mix) * 96, 16)
                    xt[pl.ds(at, 96), start : start + count] = t[p * 96 : (p + 1) * 96, :]
        start += count
    small[...] = jnp.zeros_like(small)
    cols = QUAD * HD
    width = keep.shape[1]
    for g in range(groups):
        lanes = slice(g * cols, (g + 1) * cols)
        small[0:1, lanes] = colsum(dqs[g].astype(F32))
        small[1:2, lanes] = colsum(dvs[g].astype(F32))
        tmp[0] = wo_grad[:, lanes]
        tmp[1] = mm(x0[...], dqs[g]).astype(BF)
        tmp[2] = mm(x1[...], dks[g]).astype(BF)
        tmp[3] = mm(x1[...], dvs[g]).astype(BF)
        for j in range(2):
            keep[j * width : (j + 1) * width, lanes] = tmp[j ^ info[0]]
            send[j * width : (j + 1) * width, lanes] = tmp[j ^ info[1]]
    tail = jnp.concatenate([r[...] for r in small_in] + [small[...]], axis=0).astype(BF)
    keep[2 * width :, :] = tail
    send[2 * width :, :] = tail


def weights(order, info, dqs, dks, dvs, wo_grad, pieces, smalls):
    rows = tuple(p.shape[0] for p in pieces)
    total = sum(rows)
    width = wo_grad.shape[0]
    _, tok, cols = dqs.shape
    half = pltpu.HBM((2 * width + 8 * (len(smalls) + 1), width), BF)
    count = 1 + len(smalls) + 3 + len(rows)
    return ordered(
        functools.partial(weights_body, rows, len(smalls)),
        order,
        [SM] + [VM] * count,
        (info, wo_grad, *smalls, dqs, dks, dvs, *pieces),
        "weights",
        out_specs=[VM] * 2,
        out_shape=[half, half],
        scratch_shapes=[
            pltpu.VMEM((width, tok), BF),
            pltpu.VMEM((width, total), BF),
            pltpu.VMEM((4, width, cols), BF),
            pltpu.VMEM((8, width), F32),
        ],
        cost_estimate=cost(2 * width * width * (tok + 2 * total), 4 * width * width * 4),
        compiler_params=params(),
    )


def token_body(starts, count, info, wq, wk, wv, g_sum, *refs):
    groups = HEADS // QUAD
    dqs, dks, dvs = refs[:3]
    own, outs = refs[3], refs[4:]
    cols = QUAD * HD

    def part(place):
        rows = pl.ds(place * count if isinstance(place, int) else pl.multiple_of(place * count, count), count)
        t = jnp.zeros((count, wq.shape[0]), F32)
        for g in range(groups):
            lanes = slice(g * cols, (g + 1) * cols)
            t = t + mm(dks[g, rows, :], wk[:, lanes], NT)
            t = t + mm(dvs[g, rows, :], wv[:, lanes], NT)
        return t

    t = part(0) + g_sum[...]
    for g in range(groups):
        t = t + mm(dqs[g], wq[:, g * cols : (g + 1) * cols], NT)
    own[...] = t
    for out, places in zip(outs, starts):
        for i, (base, sign) in enumerate(places):
            place = base if sign == 0 else base + sign * info[4]
            out[i * count : (i + 1) * count, :] = part(place).astype(BF)


def token_parts(order, starts, info, dqs, dks, dvs, wq, wk, wv, g_sum):
    tok, width = g_sum.shape
    return ordered(
        functools.partial(token_body, starts, tok),
        order,
        [SM] + [VM] * (4 + 3),
        (info, wq, wk, wv, g_sum, dqs, dks, dvs),
        "token_parts",
        out_specs=[VM] * (1 + len(starts)),
        out_shape=[jax.ShapeDtypeStruct((tok, width), F32)]
        + [jax.ShapeDtypeStruct((tok * len(p), width), BF) for p in starts],
        cost_estimate=cost(2 * width * width * 9 * tok, 4 * width * width * 4),
        compiler_params=params(),
    )


def unpack_body(kind, blocks, made, info, *refs):
    n = len(blocks)
    ins = refs[:n]
    refs = refs[n + made :]
    count = len(refs) - 2
    outs, wide, sems = refs[:count], refs[count], refs[count + 1]
    size = 96
    width = ins[0].shape[1]
    places = []
    for b, (ref, (side, j)) in enumerate(zip(ins, blocks)):
        for i in range(width // size):
            at = pl.multiple_of((i ^ info[5 + side]) * size, 32)
            wide[b, pl.ds(at, size), :] = ref[i * size : (i + 1) * size, :].astype(F32)
        chunk = info[side] ^ j
        if kind == "four":
            places.append([(chunk == c, outs[c]) for c in range(4)])
        else:
            at = pl.multiple_of(chunk * width, width)
            places.append([(None, outs[0].at[pl.ds(at, width), :] if kind == "rows" else outs[0].at[:, pl.ds(at, width)])])
        for when, out in places[b]:
            copy = pltpu.make_async_copy(wide.at[b], out, sems.at[b])
            if when is None:
                copy.start()
            else:
                pl.when(when)(copy.start)
    for b in range(n):
        for when, out in places[b]:
            copy = pltpu.make_async_copy(wide.at[b], out, sems.at[b])
            if when is None:
                copy.wait()
            else:
                pl.when(when)(copy.wait)


def unpack(order, kind, info, arrays, blocks, width, ff, made=()):
    shapes = {
        "rows": [(ff, width)],
        "cols": [(width, ff)],
        "four": [(width, width)] * 4,
    }[kind]
    return ordered(
        functools.partial(unpack_body, kind, blocks, len(made)),
        order,
        [SM] + [VM] * len(arrays) + [ANYWHERE] * len(made),
        (info, *arrays, *made),
        "unpack_" + kind,
        out_specs=[ANYWHERE] * len(shapes),
        out_shape=[jax.ShapeDtypeStruct(s, F32) for s in shapes],
        scratch_shapes=[pltpu.VMEM((len(arrays), width, width), F32), pltpu.SemaphoreType.DMA((len(arrays),))],
        input_output_aliases={1 + len(arrays) + i: i for i in range(len(made))},
        cost_estimate=cost(ff * width, 6 * ff * width),
        compiler_params=params(),
    )


def xor_permute(value, axis, mask):
    size = lax.axis_size(axis)
    return lax.ppermute(value, axis, [(i, i ^ mask) for i in range(size)])


def rows_at(count, index):
    return pl.BlockSpec((count, 768), lambda *_: (index, 0))


def combine_body(ways, terms, extras, *refs):
    ins, outs = refs[: ways * terms + extras], refs[ways * terms + extras :]
    for w in range(ways):
        value = ins[w * terms][...].astype(F32)
        for r in ins[w * terms + 1 : (w + 1) * terms]:
            value = value + r[...].astype(F32)
        outs[w][: value.shape[0], :] = value.astype(BF)
    if extras:
        tail = (ins[ways * terms][...].astype(F32) + ins[ways * terms + 1][...].astype(F32)).astype(BF)
        for out in outs:
            out[out.shape[0] - tail.shape[0] :, :] = tail


def combine(order, count, ways, extras=()):
    width = ways[0][0][0].shape[1]
    terms = [t for way in ways for t in way]
    made = jax.ShapeDtypeStruct((count + (32 if extras else 0), width), BF)
    return ordered(
        functools.partial(combine_body, len(ways), len(ways[0]), len(extras)),
        order,
        [rows_at(count, i) for _, i in terms] + [rows_at(32, i) for _, i in extras],
        (*(a for a, _ in terms), *(a for a, _ in extras)),
        "combine",
        grid=(1,),
        out_specs=[pl.BlockSpec(made.shape, lambda *_: (0, 0))] * len(ways),
        out_shape=[made] * len(ways),
        cost_estimate=cost(EVENT_FLOPS, 1 << 20),
        compiler_params=params(),
    )


def finish_body(parts, extras, *refs):
    ins, outs = refs[: parts + extras], refs[parts + extras :]
    value = ins[0][...].astype(F32)
    for r in ins[1:parts]:
        value = value + r[...].astype(F32)
    outs[0][...] = value.astype(BF)
    if extras:
        outs[1][...] = ins[parts][...].astype(F32) + ins[parts + 1][...].astype(F32)


def finish(order, arrays, count, extras=()):
    width = arrays[0].shape[1]
    out = [jax.ShapeDtypeStruct((count, width), BF)]
    if extras:
        out.append(jax.ShapeDtypeStruct((32, width), F32))
    return ordered(
        functools.partial(finish_body, len(arrays), len(extras)),
        order,
        [rows_at(count, 0)] * len(arrays) + [rows_at(32, i) for _, i in extras],
        (*arrays, *(a for a, _ in extras)),
        "finish",
        grid=(1,),
        out_specs=[pl.BlockSpec(o.shape, lambda *_: (0, 0)) for o in out],
        out_shape=out,
        cost_estimate=cost(EVENT_FLOPS, 1 << 20),
        compiler_params=params(),
    )


def token_sum_body(own, first, second, out):
    out[...] = own[...] + (first[...].astype(F32) + second[...].astype(F32))


def token_sum(order, own, first, second):
    tok, width = own.shape
    block = pl.BlockSpec((tok, width), lambda *_: (0, 0))
    return ordered(
        token_sum_body,
        order,
        [block] * 3,
        (own, first, second),
        "token_sum",
        grid=(1,),
        out_specs=block,
        out_shape=jax.ShapeDtypeStruct((tok, width), F32),
        cost_estimate=cost(EVENT_FLOPS, 1 << 20),
        compiler_params=params(),
    )


def stack_body(*refs):
    at = 0
    for r in refs[:-1]:
        refs[-1][at : at + r.shape[0], :] = r[...]
        at += r.shape[0]


def stack(order, arrays):
    rows, width = sum(a.shape[0] for a in arrays), arrays[0].shape[1]
    return ordered(
        stack_body,
        order,
        [VM] * len(arrays),
        (*arrays,),
        "stack",
        out_specs=VM,
        out_shape=jax.ShapeDtypeStruct((rows, width), arrays[0].dtype),
        cost_estimate=cost(EVENT_FLOPS, 1 << 20),
        compiler_params=params(),
    )


STAGES = (((1, 0), (2, 0)), ((2, 0), (1, 0)), ((0, 2), (0, 4)), ((0, 4), (0, 2)))


def swap(value, stage):
    shards = lax.axis_size("seq")
    pairs = []
    for b in range(lax.axis_size("batch")):
        of_shard, of_batch = STAGES[stage][b % 2]
        pairs += [(b * shards + s, (b ^ of_batch) * shards + (s ^ of_shard)) for s in range(shards)]
    return lax.ppermute(value, ("batch", "seq"), pairs)


class Order:
    def __init__(self):
        self.last = None


class Unit:
    def __init__(self, order, keep, got, rows):
        self.order, self.rows, self.stage = order, rows, 0
        self.parts = [keep, got]
        self.extra = [(a, rows // 32) for a in self.parts] if keep.shape[0] > rows else []

    def step(self):
        if self.stage < 4:
            half = self.rows // 2
            (sent,) = combine(self.order, half, [[(p, 1) for p in self.parts]], self.extra)
            got = swap(sent, self.stage)
            if self.extra:
                self.extra = [(sent, half // 32), (got, half // 32)]
            self.parts.append(got)
            self.rows = half
        else:
            if self.stage == 4:
                body, *tail = finish(self.order, self.parts, self.rows, self.extra)
                self.extra = tail[0] if tail else None
            else:
                body = stack(self.order, self.held)
            self.held = [body, swap(body, 7 - self.stage)]
        self.stage += 1

    def forward(self):
        self.others = [xor_permute(a, "batch", 1) for a in self.held]


def summed_plain(info, first, second, third, tokens, width, ff):
    axes = ("batch", "seq")

    def whole_sum(keep, send):
        part = lax.psum_scatter(jnp.concatenate([keep, send], axis=0), axes, scatter_dimension=0, tiled=True)
        return lax.all_gather(part, axes, axis=0, tiled=True)

    blocks = ((0, 0), (0, 1), (1, 0), (1, 1))

    def placed(kind, pair):
        total = whole_sum(*pair)
        return unpack(None, kind, info, [total[i * width : (i + 1) * width] for i in range(4)], blocks, width, ff)

    d_outer = placed("rows", first)
    d_inner = placed("cols", second)
    d_four = placed("four", third)
    return d_outer, d_inner, d_four, [xor_permute(t, "seq", k) for k, t in enumerate(tokens, 1)]


def gather_tokens(x, small):
    size = lax.axis_size("seq")
    if small:
        a = xor_permute(x, "seq", 1)
        b = xor_permute(x, "seq", 2)
        half = x.shape[0] // 2
        return [x, a, b, xor_permute(a[:half], "seq", 2), xor_permute(b[half:], "seq", 1)]
    return [x] + [xor_permute(x, "seq", k) for k in range(1, size)]


def multiplicity_bias(random_blocks, count, shard_index, shard_count, blocks_dev):
    order = shard_index ^ jnp.arange(shard_count, dtype=jnp.int32)
    key_ids = (order[:, None] * blocks_dev + jnp.arange(blocks_dev, dtype=jnp.int32)[None, :]).reshape(-1)
    query_ids = shard_index * blocks_dev + jnp.arange(blocks_dev, dtype=jnp.int32)
    near = (jnp.abs(key_ids[:, None] - query_ids[None, :]) <= 1).astype(jnp.int32)
    lead = (key_ids < count).astype(jnp.int32)
    picks = random_blocks.transpose(1, 0, 2)
    times = jnp.sum((picks[:, None, :, :] == key_ids[None, :, None, None]).astype(jnp.int32), axis=-1)
    times = times + near[None] + lead[None, :, None]
    times = jnp.where((query_ids < count)[None, None, :], 1, times)
    bias = jnp.where(times > 0, jnp.log(jnp.maximum(times, 1).astype(F32)), NEGATIVE)
    return jnp.repeat(bias, BLK, axis=2)


def on_device(
    tokens, cotangent, w_query, b_query, w_key, w_value, b_value, w_out, b_out, first_gain, first_shift,
    w_inner, b_inner, w_outer, b_outer, second_gain, second_shift, global_counts, random_blocks,
):
    _, tok, width = tokens.shape
    ff = w_inner.shape[1]
    blocks_dev = tok // BLK
    shard_count = lax.axis_size("seq")
    shard = lax.axis_index("seq")
    batch = lax.axis_index("batch")
    direct = shard_count == 4 and lax.axis_size("batch") == 8
    if direct:
        core, z = batch & 1, batch >> 1
        x_bit, y_bit = shard & 1, shard >> 1
        first = jnp.where(core == 0, x_bit, y_bit)
        low_z, high_z = z & 1, z >> 1
        mix_0, mix_1 = y_bit * 4 + low_z * 2 + high_z, x_bit * 4 + high_z * 2 + low_z
        info = [core * 2 + first, (1 - core) * 2 + (x_bit + y_bit - first), mix_0, mix_1, core]
        info += [jnp.where(core == 0, mix_0, mix_1), jnp.where(core == 0, mix_1, mix_0)]
        info = jnp.stack(info).astype(jnp.int32)
    else:
        info = jnp.array([0, 2, 0, 0, 0, 0, 0], jnp.int32)
    x = tokens.reshape(tok, width)
    vec = jnp.concatenate(
        [b_query, b_value, b_out, first_gain, first_shift, b_outer, second_gain, second_shift, b_inner]
    ).reshape(-1, width)
    bias = multiplicity_bias(random_blocks[0], global_counts[0], shard, shard_count, blocks_dev)
    pieces = gather_tokens(x, direct)
    rows = tuple(p.shape[0] for p in pieces)
    groups = HEADS // QUAD
    order = Order() if direct else None
    pairs = ((0, 0), (0, 1), (1, 0), (1, 1))
    q, k, v, o, lse = attend(order, pieces, w_query, w_key, w_value, vec, bias)
    layer_out, u1, r1, g_second, g_outer, slope, small_1, hid_t, send_1 = feed(
        order, info, o, x, cotangent.reshape(tok, width), w_out, w_inner, w_outer, vec
    )

    def exchange(value):
        return xor_permute(value, "batch", 1) if direct else value

    got_1 = exchange(send_1)
    keep_1, g_in, low_t, back, small_2, send_2 = inner_back(
        order, info, u1, g_second, g_outer, slope, hid_t, w_inner, w_outer, vec
    )
    if direct:
        one = Unit(order, keep_1, got_1, 2 * width)
        one.step()
    keep_2, g_sum, g_att, dots, small_3, wo_grad = branch_back(order, info, o, u1, r1, back, g_in, low_t, w_out, vec)
    dots = dots[:HEADS].reshape(groups, QUAD, tok)
    got_2 = exchange(send_2)

    def attend_step():
        return attend_back(order, q, k, v, g_att, bias, lse, dots)

    def weights_step():
        return weights(order, info, *backs, wo_grad, pieces, smalls)

    def token_step(starts):
        return token_parts(order, starts, info, *backs, w_query, w_key, w_value, g_sum)

    smalls = (small_1, small_2, small_3)
    if direct:
        two = Unit(order, keep_2, got_2, 2 * width)
        two.step()
        backs = attend_step()
        one.step()
        keep_3, send_3 = weights_step()
        three = Unit(order, keep_3, exchange(send_3), 2 * width)
        two.step()
        one.step()
        parts = token_step((((1, 1), (3, 0)), ((2, -1),)))
        got_a = swap(parts[1], 0)
        two.step()
        one.step()
        three.step()
        two.step()
        one.step()
        (relay,) = combine(order, tok, [[(parts[2], 0), (got_a, 1)]])
        got_b = swap(relay, 1)
        two.step()
        one.step()
        three.step()
        token_grad = token_sum(order, parts[0], got_a, got_b)
        two.step()
        one.step()
        three.step()
        two.step()
        one.step()
        three.step()
        two.step()
        three.step()
        three.step()
        one.forward()
        (d_outer,) = unpack(order, "rows", info, one.held + one.others, pairs, width, ff)
        three.step()
        two.forward()
        (d_inner,) = unpack(order, "cols", info, two.held + two.others, pairs, width, ff)
        three.step()
        three.others = [xor_permute(three.held[0], "batch", 1)]
        made = unpack(order, "four", info, [three.held[0], three.others[0]], pairs[::2], width, ff)
        three.held[1], *made = lax.optimization_barrier((three.held[1], *made))
        three.others.append(xor_permute(three.held[1], "batch", 1))
        made = unpack(order, "four", info, [three.held[1]], pairs[1:2], width, ff, made)
        d_out, d_query, d_key, d_value = unpack(order, "four", info, [three.others[1]], pairs[3:], width, ff, made)
        vectors = three.extra
    else:
        backs = attend_step()
        keep_3, send_3 = weights_step()
        parts = token_step(tuple(((i, 0),) for i in range(1, shard_count)))
        vectors = lax.psum(keep_3[2 * width :].astype(F32), ("batch", "seq"))
        third = (keep_3[: 2 * width], send_3[: 2 * width])
        d_outer, d_inner, d_four, got = summed_plain(
            info, (keep_1, send_1), (keep_2, send_2), third, parts[1:], width, ff
        )
        (d_outer,), (d_inner,) = d_outer, d_inner
        d_out, d_query, d_key, d_value = d_four
        token_grad = sum([g.astype(F32) for g in got], parts[0])
    return (
        layer_out.reshape(1, tok, width),
        token_grad.reshape(1, tok, width),
        d_query,
        vectors[24],
        d_key,
        d_value,
        vectors[25],
        d_out,
        vectors[16],
        vectors[17],
        vectors[18],
        d_inner,
        vectors[8:12].reshape(-1),
        d_outer,
        vectors[3],
        vectors[4],
        vectors[5],
    )


def solution(mesh):
    token_spec = P("batch", "seq", None)
    placed = (token_spec, token_spec) + (P(),) * 15 + (P("batch"), P("batch", "seq", None, None))
    return jax.shard_map(
        on_device,
        mesh=mesh,
        in_specs=placed,
        out_specs=(token_spec, token_spec) + (P(),) * 15,
        check_vma=False,
    )
```

profile of v0, /device:TPU:0, one launch (start us, length us, event | category | flops | bytes accessed | tf_op | source)
XLA Modules:
  0.0 234.5 jit_solution(18137477545578867272)
XLA Ops:
  0.7 3.0 %collective-permute-start.1 = (bf16[256,768]{1,0:T(8,128)(2,1)}, bf16[256,768]{1,0:T(8,128)(2,1)S(1)}, u32[]{:S(2)}, u32[]{:S(2)}) collective-permute-start(bf16[256,768]{1,0:T(8,128)(2,1)} %bitcast.20), channel_id=1, source_target_pairs={{0,2},{1,3},{2,0},{3,1},{4,6},{5,7},{6,4},{7,5},{8,10},{9,11},{10,... | collective-permute-start | bytes 1179656 | tf_op jit(solution)/shard_map/ppermute | solution.py:605
  20.6 12.4 %attend.1 = (bf16[256,768]{1,0:T(8,128)(2,1)}, bf16[3,1024,256]{2,1,0:T(8,128)(2,1)}, bf16[3,1024,256]{2,1,0:T(8,128)(2,1)}, f32[256,768]{1,0:T(8,128)S(1)}, f32...) custom-call(bf16[256,768]{1,0:T(8,128)(2,1)S(1)} %bitcast.22, bf16[256,768]{1,0:T(8,128)(2,1)S(1)} %collective-permute-done.refs_1_.refs_9_, ...), custom_call_target="tpu_custom_call" | custom-call | flops 563714457600 | bytes 629145600 | tf_op jit(solution)/shard_map/attend/pallas_call | solution.py:57
  33.1 9.2 %feed.1 = (bf16[256,768]{1,0:T(8,128)(2,1)}, f32[256,768]{1,0:T(8,128)S(1)}, f32[256,128]{1,0:T(8,128)S(1)}, f32[256,768]{1,0:T(8,128)S(1)}, bf16[256,768]{1,0:T...) custom-call(s32[7]{0:T(128)S(1)} %stack.40.refs_0_, ...), custom_call_target="tpu_custom_call" | custom-call | flops 332188876800 | bytes 1887436800 | tf_op jit(solution)/shard_map/feed/pallas_call | solution.py:57
  42.4 7.3 %inner_back.1 = (bf16[1536,768]{1,0:T(8,128)(2,1)}, bf16[256,3072]{1,0:T(8,128)(2,1)S(1)}, bf16[2,768,256]{2,1,0:T(8,128)(2,1)S(1)}, f32[256,768]{1,0:T(8,128)S(...) custom-call(s32[7]{0:T(128)S(1)} %stack.40.refs_0_, ...), custom_call_target="tpu_custom_call" | custom-call | flops 362387865600 | bytes 1887436800 | tf_op jit(solution)/shard_map/inner_back/pallas_call | solution.py:57
  54.6 4.3 %branch_back.1 = (bf16[1536,768]{1,0:T(8,128)(2,1)}, f32[256,768]{1,0:T(8,128)}, bf16[256,768]{1,0:T(8,128)(2,1)}, f32[16,256]{1,0:T(8,128)S(1)}, f32[8,768]{1,0...) custom-call(s32[7]{0:T(128)S(1)} %stack.40.refs_0_, f32[256,768]{1,0:T(8,128)S(1)} %copy-done.28, ...), custom_call_target="tpu_custom_call" | custom-call | flops 120795955200 | bytes 943718400 | tf_op jit(solution)/shard_map/branch_back/pallas_call | solution.py:57
  63.9 13.2 %attend_back.1 = (bf16[3,256,256]{2,1,0:T(8,128)(2,1)S(1)}, bf16[3,1024,256]{2,1,0:T(8,128)(2,1)S(1)}, bf16[3,1024,256]{2,1,0:T(8,128)(2,1)S(1)}, f32[8,128]{1,0:T(8,128)S(1)}) custom-call(bf16[256,768]{1,0:T(8,128)(2,1)} %get-tuple-element.152.refs_0_, bf16[3,1024,256]{2,1,0:T(8,128)(2,1)} %get-tuple-element.153.refs_1_, ...), custom_call_target="tpu_custom_call" | custom-call | flops 805306368000 | bytes 629145600 | tf_op jit(solution)/shard_map/attend_back/pallas_call | solution.py:57
  81.2 6.7 %weights.1 = (bf16[1568,768]{1,0:T(8,128)(2,1)}, bf16[1568,768]{1,0:T(8,128)(2,1)}, f32[8,128]{1,0:T(8,128)S(1)}) custom-call(s32[7]{0:T(128)S(1)} %stack.40.refs_0_, bf16[768,768]{1,0:T(8,128)(2,1)S(1)} %copy-done.25, f32[8,768]{1,0:T(8,128)S(1)} %get-tuple-element.170.refs_2_, f32[8,768]{1,0:T(8,128)S(1)} %get-tuple-element.171.refs_3_, ...), custom_call_target="tpu_custom_call" | custom-call | flops 271790899200 | bytes 943718400 | tf_op jit(solution)/shard_map/weights/pallas_call | solution.py:57
  87.9 6.1 %collective-permute-done.8.refs_2_ = bf16[768,768]{1,0:T(8,128)(2,1)} collective-permute-done((bf16[768,768]{1,0:T(8,128)(2,1)}, bf16[768,768]{1,0:T(8,128)(2,1)}, u32[]{:S(2)}, u32[]{:S(2)}) %collective-permute-start.8) | collective-permute-done | bytes 1179680 | tf_op jit(solution)/shard_map/ppermute | solution.py:724
  101.6 3.5 %token_parts.1 = (f32[256,768]{1,0:T(8,128)S(1)}, bf16[512,768]{1,0:T(8,128)(2,1)S(1)}, bf16[256,768]{1,0:T(8,128)(2,1)S(1)}, f32[8,128]{1,0:T(8,128)S(1)}) custom-call(s32[7]{0:T(128)S(1)} %stack.40.refs_0_, bf16[768,768]{1,0:T(8,128)(2,1)S(1)} %copy-done.5, bf16[768,768]{1,0:T(8,128)(2,1)S(1)} %copy-done.6, bf16[768,768]{1,0:T(8,128)(2,1)S(1)} %copy-done.7, ...), custom_call_target="tpu_custom_call" | custom-call | flops 271790899200 | bytes 943718400 | tf_op jit(solution)/shard_map/token_parts/pallas_call | solution.py:57
  116.3 3.8 %collective-permute-done.13.refs_4_ = bf16[192,768]{1,0:T(8,128)(2,1)S(1)} collective-permute-done((bf16[192,768]{1,0:T(8,128)(2,1)S(1)}, bf16[192,768]{1,0:T(8,128)(2,1)S(1)}, u32[]{:S(2)}, u32[]{:S(2)}) %collective-permute-start.13) | collective-permute-done | bytes 294944 | tf_op jit(solution)/shard_map/ppermute | solution.py:724
  127.8 6.3 %collective-permute-done.18.refs_5_ = bf16[96,768]{1,0:T(8,128)(2,1)S(1)} collective-permute-done((bf16[96,768]{1,0:T(8,128)(2,1)S(1)}, bf16[96,768]{1,0:T(8,128)(2,1)S(1)}, u32[]{:S(2)}, u32[]{:S(2)}) %collective-permute-start.18) | collective-permute-done | bytes 147488 | tf_op jit(solution)/shard_map/ppermute | solution.py:724
  135.3 3.5 %collective-permute-start.20 = (bf16[192,768]{1,0:T(8,128)(2,1)S(1)}, bf16[192,768]{1,0:T(8,128)(2,1)S(1)}, u32[]{:S(2)}, u32[]{:S(2)}) collective-permute-start(bf16[192,768]{1,0:T(8,128)(2,1)S(1)} %get-tuple-element.202.refs_0_), channel_id=1, source_target_pairs={{0,8},{1,9},{2,10},{3,11},{4,20},{5,21},{6,22},{7,23},{8,0},{9,1},... | collective-permute-start | bytes 884744 | tf_op jit(solution)/shard_map/ppermute | solution.py:724
  138.9 5.3 %collective-permute-done.16.refs_2_.refs_4_ = bf16[800,768]{1,0:T(8,128)(2,1)S(1)} collective-permute-done((bf16[800,768]{1,0:T(8,128)(2,1)S(1)}, bf16[800,768]{1,0:T(8,128)(2,1)S(1)}, u32[]{:S(2)}, u32[]{:S(2)}) %collective-permute-start.16) | collective-permute-done | bytes 1228832 | tf_op jit(solution)/shard_map/ppermute | solution.py:724
  149.2 6.7 %collective-permute-done.19.refs_3_.refs_5_ = bf16[416,768]{1,0:T(8,128)(2,1)S(1)} collective-permute-done((bf16[416,768]{1,0:T(8,128)(2,1)S(1)}, bf16[416,768]{1,0:T(8,128)(2,1)S(1)}, u32[]{:S(2)}, u32[]{:S(2)}) %collective-permute-start.19) | collective-permute-done | bytes 639008 | tf_op jit(solution)/shard_map/ppermute | solution.py:724
  157.5 4.7 %collective-permute-done.23.refs_1_ = bf16[384,768]{1,0:T(8,128)(2,1)S(1)} collective-permute-done((bf16[384,768]{1,0:T(8,128)(2,1)S(1)}, bf16[384,768]{1,0:T(8,128)(2,1)S(1)}, u32[]{:S(2)}, u32[]{:S(2)}) %collective-permute-start.23) | collective-permute-done | bytes 589856 | tf_op jit(solution)/shard_map/ppermute | solution.py:724
  166.7 4.2 %collective-permute-start.25 = (bf16[128,768]{1,0:T(8,128)(2,1)S(1)}, bf16[128,768]{1,0:T(8,128)(2,1)S(1)}, u32[]{:S(2)}, u32[]{:S(2)}) collective-permute-start(bf16[128,768]{1,0:T(8,128)(2,1)S(1)} %get-tuple-element.213.refs_6_), channel_id=1, source_target_pairs={{0,16},{1,17},{2,18},{3,19},{4,12},{5,13},{6,14},{7,15},{8,24},{9,... | collective-permute-start | bytes 589832 | tf_op jit(solution)/shard_map/ppermute | solution.py:724
  170.9 8.9 %collective-permute-done.26.refs_1_ = bf16[384,768]{1,0:T(8,128)(2,1)S(1)} collective-permute-done((bf16[384,768]{1,0:T(8,128)(2,1)S(1)}, bf16[384,768]{1,0:T(8,128)(2,1)S(1)}, u32[]{:S(2)}, u32[]{:S(2)}) %collective-permute-start.26) | collective-permute-done | bytes 589856 | tf_op jit(solution)/shard_map/ppermute | solution.py:724
  184.0 3.6 %collective-permute-start.27 = (bf16[96,768]{1,0:T(8,128)(2,1)S(1)}, bf16[96,768]{1,0:T(8,128)(2,1)S(1)}, u32[]{:S(2)}, u32[]{:S(2)}) collective-permute-start(bf16[96,768]{1,0:T(8,128)(2,1)S(1)} %get-tuple-element.217.refs_0_), channel_id=1, source_target_pairs={{0,16},{1,17},{2,18},{3,19},{4,12},{5,13},{6,14},{7,15},{8,24},{9,... | collective-permute-start | bytes 442376 | tf_op jit(solution)/shard_map/ppermute | solution.py:724
  187.7 3.6 %collective-permute-done.27.refs_1_ = bf16[96,768]{1,0:T(8,128)(2,1)S(1)} collective-permute-done((bf16[96,768]{1,0:T(8,128)(2,1)S(1)}, bf16[96,768]{1,0:T(8,128)(2,1)S(1)}, u32[]{:S(2)}, u32[]{:S(2)}) %collective-permute-start.27) | collective-permute-done | bytes 147488 | tf_op jit(solution)/shard_map/ppermute | solution.py:724
  196.1 4.4 %unpack_rows.1 = (f32[3072,768]{1,0:T(8,128)}, f32[8,128]{1,0:T(8,128)S(1)}) custom-call(s32[7]{0:T(128)S(1)} %stack.40.refs_0_, bf16[768,768]{1,0:T(8,128)(2,1)S(1)} %get-tuple-element.220.refs_1_, bf16[768,768]{1,0:T(8,128)(2,1)S(1)} %collective-permute-done.29.refs_2_, bf16[768,768]{1,0:T(8,128)(2,1)S(1)} %collective-permute-done.30.refs_3_, ...), custom_call_target="tpu_custom_call" | custom-call | flops 235929600 | bytes 1415577600 | tf_op jit(solution)/shard_map/unpack_rows/pallas_call | solution.py:57
  202.7 4.4 %unpack_cols.1 = (f32[768,3072]{1,0:T(8,128)}, f32[8,128]{1,0:T(8,128)S(1)}) custom-call(s32[7]{0:T(128)S(1)} %stack.40.refs_0_, bf16[768,768]{1,0:T(8,128)(2,1)S(1)} %get-tuple-element.224.refs_1_, bf16[768,768]{1,0:T(8,128)(2,1)S(1)} %collective-permute-done.33.refs_2_, bf16[768,768]{1,0:T(8,128)(2,1)S(1)} %collective-permute-done.34.refs_3_, ...), custom_call_target="tpu_custom_call" | custom-call | flops 235929600 | bytes 1415577600 | tf_op jit(solution)/shard_map/unpack_cols/pallas_call | solution.py:57
  207.1 4.7 %collective-permute-done.32.refs_1_ = bf16[384,768]{1,0:T(8,128)(2,1)S(1)} collective-permute-done((bf16[384,768]{1,0:T(8,128)(2,1)S(1)}, bf16[384,768]{1,0:T(8,128)(2,1)S(1)}, u32[]{:S(2)}, u32[]{:S(2)}) %collective-permute-start.32) | collective-permute-done | bytes 589856 | tf_op jit(solution)/shard_map/ppermute | solution.py:724
  214.8 2.9 %unpack_four.3 = (f32[768,768]{1,0:T(8,128)}, f32[768,768]{1,0:T(8,128)}, f32[768,768]{1,0:T(8,128)}, f32[768,768]{1,0:T(8,128)}, f32[8,128]{1,0:T(8,128)S(1)}) custom-call(s32[7]{0:T(128)S(1)} %copy-done.1, bf16[768,768]{1,0:T(8,128)(2,1)S(1)} %get-tuple-element.227.refs_1_, bf16[768,768]{1,0:T(8,128)(2,1)S(1)} %collective-permute-done.37.refs_2_, ...), custom_call_target="tpu_custom_call" | custom-call | flops 235929600 | bytes 1415577600 | tf_op jit(solution)/shard_map/unpack_four/pallas_call | solution.py:57
  217.7 10.5 %collective-permute-done.36.refs_1_ = bf16[768,768]{1,0:T(8,128)(2,1)S(1)} collective-permute-done((bf16[768,768]{1,0:T(8,128)(2,1)S(1)}, bf16[768,768]{1,0:T(8,128)(2,1)S(1)}, u32[]{:S(2)}, u32[]{:S(2)}) %collective-permute-start.36) | collective-permute-done | bytes 1179680 | tf_op jit(solution)/shard_map/ppermute | solution.py:724
  (181 shorter events, 89.1 us)
Async XLA Ops:
  0.7 12.6 %collective-permute-start.1 = (bf16[256,768]{1,0:T(8,128)(2,1)}, bf16[256,768]{1,0:T(8,128)(2,1)S(1)}, u32[]{:S(2)}, u32[]{:S(2)}) collective-permute-start(bf16[256,768]{1,0:T(8,128)(2,1)} %bitcast.20), channel_id=1, source_target_pairs={{0,2},{1,3},{2,0},{3,1},{4,6},{5,7},{6,4},{7,5},{8,10},{9,11},{10,... | collective-permute-start | bytes 1179656 | tf_op jit(solution)/shard_map/ppermute | solution.py:605
  3.7 11.1 %collective-permute-start = (bf16[256,768]{1,0:T(8,128)(2,1)}, bf16[256,768]{1,0:T(8,128)(2,1)S(1)}, u32[]{:S(2)}, u32[]{:S(2)}) collective-permute-start(bf16[256,768]{1,0:T(8,128)(2,1)} %bitcast.21), channel_id=1, source_target_pairs={{0,1},{1,0},{2,3},{3,2},{4,5},{5,4},{6,7},{7,6},{8,9},{9,8},{10,11... | collective-permute-start | bytes 1179656 | tf_op jit(solution)/shard_map/ppermute | solution.py:605
  58.9 18.2 %collective-permute-start.6 = (bf16[768,768]{1,0:T(8,128)(2,1)}, bf16[768,768]{1,0:T(8,128)(2,1)}, u32[]{:S(2)}, u32[]{:S(2)}) collective-permute-start(bf16[768,768]{1,0:T(8,128)(2,1)} %copy-done.8), channel_id=1, source_target_pairs={{0,1},{1,0},{2,3},{3,2},{4,6},{5,7},{6,4},{7,5},{8,9},{9,8},{10,11... | collective-permute-start | bytes 3538952 | tf_op jit(solution)/shard_map/ppermute | solution.py:724
  63.1 31.0 %collective-permute-start.8 = (bf16[768,768]{1,0:T(8,128)(2,1)}, bf16[768,768]{1,0:T(8,128)(2,1)}, u32[]{:S(2)}, u32[]{:S(2)}) collective-permute-start(bf16[768,768]{1,0:T(8,128)(2,1)} %get-tuple-element.168), channel_id=1, source_target_pairs={{0,1},{1,0},{2,3},{3,2},{4,6},{5,7},{6,4},{7,5},{8,9},{9,8},{10,11... | collective-permute-start | bytes 3538952 | tf_op jit(solution)/shard_map/ppermute | solution.py:724
  79.6 18.2 %collective-permute-start.7 = (bf16[384,768]{1,0:T(8,128)(2,1)}, bf16[384,768]{1,0:T(8,128)(2,1)}, u32[]{:S(2)}, u32[]{:S(2)}) collective-permute-start(bf16[384,768]{1,0:T(8,128)(2,1)} %get-tuple-element.167), channel_id=1, source_target_pairs={{0,2},{1,3},{2,0},{3,1},{4,5},{5,4},{6,7},{7,6},{8,10},{9,11},{10,... | collective-permute-start | bytes 1769480 | tf_op jit(solution)/shard_map/ppermute | solution.py:724
  97.8 16.9 %collective-permute-start.14 = (bf16[1568,768]{1,0:T(8,128)(2,1)}, bf16[1568,768]{1,0:T(8,128)(2,1)}, u32[]{:S(2)}, u32[]{:S(2)}) collective-permute-start(bf16[1568,768]{1,0:T(8,128)(2,1)} %get-tuple-element.187), channel_id=1, source_target_pairs={{0,4},{4,0},{8,12},{12,8},{16,20},{20,16},{24,28},{28,24},{1,5},{5... | collective-permute-start | bytes 7225352 | tf_op jit(solution)/shard_map/ppermute | solution.py:605
  100.0 10.6 %collective-permute-start.10 = (bf16[192,768]{1,0:T(8,128)(2,1)}, bf16[192,768]{1,0:T(8,128)(2,1)}, u32[]{:S(2)}, u32[]{:S(2)}) collective-permute-start(bf16[192,768]{1,0:T(8,128)(2,1)} %get-tuple-element.180), channel_id=1, source_target_pairs={{0,8},{1,9},{2,10},{3,11},{4,20},{5,21},{6,22},{7,23},{8,0},{9,1},... | collective-permute-start | bytes 884744 | tf_op jit(solution)/shard_map/ppermute | solution.py:724
  107.9 12.2 %collective-permute-start.13 = (bf16[192,768]{1,0:T(8,128)(2,1)S(1)}, bf16[192,768]{1,0:T(8,128)(2,1)S(1)}, u32[]{:S(2)}, u32[]{:S(2)}) collective-permute-start(bf16[192,768]{1,0:T(8,128)(2,1)S(1)} %get-tuple-element.185), channel_id=1, source_target_pairs={{0,8},{1,9},{2,10},{3,11},{4,20},{5,21},{6,22},{7,23},{8,0},{9,1},... | collective-permute-start | bytes 884744 | tf_op jit(solution)/shard_map/ppermute | solution.py:724
  109.5 17.2 %collective-permute-start.9 = (bf16[512,768]{1,0:T(8,128)(2,1)S(1)}, bf16[512,768]{1,0:T(8,128)(2,1)S(1)}, u32[]{:S(2)}, u32[]{:S(2)}) collective-permute-start(bf16[512,768]{1,0:T(8,128)(2,1)S(1)} %get-tuple-element.178), channel_id=1, source_target_pairs={{0,1},{1,0},{2,3},{3,2},{4,6},{5,7},{6,4},{7,5},{8,9},{9,8},{10,11... | collective-permute-start | bytes 2359304 | tf_op jit(solution)/shard_map/ppermute | solution.py:724
  122.4 12.8 %collective-permute-start.17 = (bf16[96,768]{1,0:T(8,128)(2,1)S(1)}, bf16[96,768]{1,0:T(8,128)(2,1)S(1)}, u32[]{:S(2)}, u32[]{:S(2)}) collective-permute-start(bf16[96,768]{1,0:T(8,128)(2,1)S(1)} %get-tuple-element.194.refs_0_), channel_id=1, source_target_pairs={{0,16},{1,17},{2,18},{3,19},{4,12},{5,13},{6,14},{7,15},{8,24},{9,... | collective-permute-start | bytes 442376 | tf_op jit(solution)/shard_map/ppermute | solution.py:724
  125.4 18.7 %collective-permute-start.16 = (bf16[800,768]{1,0:T(8,128)(2,1)S(1)}, bf16[800,768]{1,0:T(8,128)(2,1)S(1)}, u32[]{:S(2)}, u32[]{:S(2)}) collective-permute-start(bf16[800,768]{1,0:T(8,128)(2,1)S(1)} %get-tuple-element.193.refs_3_), channel_id=1, source_target_pairs={{0,1},{1,0},{2,3},{3,2},{4,6},{5,7},{6,4},{7,5},{8,9},{9,8},{10,11... | collective-permute-start | bytes 3686408 | tf_op jit(solution)/shard_map/ppermute | solution.py:724
  126.8 20.1 %collective-permute-start.15 = (bf16[256,768]{1,0:T(8,128)(2,1)S(1)}, bf16[256,768]{1,0:T(8,128)(2,1)S(1)}, u32[]{:S(2)}, u32[]{:S(2)}) collective-permute-start(bf16[256,768]{1,0:T(8,128)(2,1)S(1)} %get-tuple-element.192), channel_id=1, source_target_pairs={{0,2},{1,3},{2,0},{3,1},{4,5},{5,4},{6,7},{7,6},{8,10},{9,11},{10,... | collective-permute-start | bytes 1179656 | tf_op jit(solution)/shard_map/ppermute | solution.py:724
  135.2 12.7 %collective-permute-start.21 = (bf16[96,768]{1,0:T(8,128)(2,1)S(1)}, bf16[96,768]{1,0:T(8,128)(2,1)S(1)}, u32[]{:S(2)}, u32[]{:S(2)}) collective-permute-start(bf16[96,768]{1,0:T(8,128)(2,1)S(1)} %get-tuple-element.203.refs_0_), channel_id=1, source_target_pairs={{0,16},{1,17},{2,18},{3,19},{4,12},{5,13},{6,14},{7,15},{8,24},{9,... | collective-permute-start | bytes 442376 | tf_op jit(solution)/shard_map/ppermute | solution.py:724
  135.3 13.4 %collective-permute-start.20 = (bf16[192,768]{1,0:T(8,128)(2,1)S(1)}, bf16[192,768]{1,0:T(8,128)(2,1)S(1)}, u32[]{:S(2)}, u32[]{:S(2)}) collective-permute-start(bf16[192,768]{1,0:T(8,128)(2,1)S(1)} %get-tuple-element.202.refs_0_), channel_id=1, source_target_pairs={{0,8},{1,9},{2,10},{3,11},{4,20},{5,21},{6,22},{7,23},{8,0},{9,1},... | collective-permute-start | bytes 884744 | tf_op jit(solution)/shard_map/ppermute | solution.py:724
  145.4 10.5 %collective-permute-start.19 = (bf16[416,768]{1,0:T(8,128)(2,1)S(1)}, bf16[416,768]{1,0:T(8,128)(2,1)S(1)}, u32[]{:S(2)}, u32[]{:S(2)}) collective-permute-start(bf16[416,768]{1,0:T(8,128)(2,1)S(1)} %get-tuple-element.201.refs_4_), channel_id=1, source_target_pairs={{0,2},{1,3},{2,0},{3,1},{4,5},{5,4},{6,7},{7,6},{8,10},{9,11},{10,... | collective-permute-start | bytes 1916936 | tf_op jit(solution)/shard_map/ppermute | solution.py:724
  148.8 13.4 %collective-permute-start.23 = (bf16[384,768]{1,0:T(8,128)(2,1)S(1)}, bf16[384,768]{1,0:T(8,128)(2,1)S(1)}, u32[]{:S(2)}, u32[]{:S(2)}) collective-permute-start(bf16[384,768]{1,0:T(8,128)(2,1)S(1)} %get-tuple-element.208.refs_0_), channel_id=1, source_target_pairs={{0,2},{1,3},{2,0},{3,1},{4,5},{5,4},{6,7},{7,6},{8,10},{9,11},{10,... | collective-permute-start | bytes 1769480 | tf_op jit(solution)/shard_map/ppermute | solution.py:724
  162.3 20.7 %collective-permute-start.29 = (bf16[768,768]{1,0:T(8,128)(2,1)S(1)}, bf16[768,768]{1,0:T(8,128)(2,1)S(1)}, u32[]{:S(2)}, u32[]{:S(2)}) collective-permute-start(bf16[768,768]{1,0:T(8,128)(2,1)S(1)} %get-tuple-element.220.refs_1_), channel_id=1, source_target_pairs={{0,1},{1,0},{2,3},{3,2},{4,6},{5,7},{6,4},{7,5},{8,9},{9,8},{10,11... | collective-permute-start | bytes 3538952 | tf_op jit(solution)/shard_map/ppermute | solution.py:724
  163.5 16.3 %collective-permute-start.26 = (bf16[384,768]{1,0:T(8,128)(2,1)S(1)}, bf16[384,768]{1,0:T(8,128)(2,1)S(1)}, u32[]{:S(2)}, u32[]{:S(2)}) collective-permute-start(bf16[384,768]{1,0:T(8,128)(2,1)S(1)} %get-tuple-element.214.refs_0_), channel_id=1, source_target_pairs={{0,2},{1,3},{2,0},{3,1},{4,5},{5,4},{6,7},{7,6},{8,10},{9,11},{10,... | collective-permute-start | bytes 1769480 | tf_op jit(solution)/shard_map/ppermute | solution.py:724
  164.3 31.7 %collective-permute-start.30 = (bf16[768,768]{1,0:T(8,128)(2,1)S(1)}, bf16[768,768]{1,0:T(8,128)(2,1)S(1)}, u32[]{:S(2)}, u32[]{:S(2)}) collective-permute-start(bf16[768,768]{1,0:T(8,128)(2,1)S(1)} %get-tuple-element.220.refs_1_), channel_id=1, source_target_pairs={{0,4},{4,0},{8,12},{12,8},{16,20},{20,16},{24,28},{28,24},{1,5},{5... | collective-permute-start | bytes 3538952 | tf_op jit(solution)/shard_map/ppermute | solution.py:605
  166.7 16.3 %collective-permute-start.25 = (bf16[128,768]{1,0:T(8,128)(2,1)S(1)}, bf16[128,768]{1,0:T(8,128)(2,1)S(1)}, u32[]{:S(2)}, u32[]{:S(2)}) collective-permute-start(bf16[128,768]{1,0:T(8,128)(2,1)S(1)} %get-tuple-element.213.refs_6_), channel_id=1, source_target_pairs={{0,16},{1,17},{2,18},{3,19},{4,12},{5,13},{6,14},{7,15},{8,24},{9,... | collective-permute-start | bytes 589832 | tf_op jit(solution)/shard_map/ppermute | solution.py:724
  179.8 16.3 %collective-permute-start.33 = (bf16[768,768]{1,0:T(8,128)(2,1)S(1)}, bf16[768,768]{1,0:T(8,128)(2,1)S(1)}, u32[]{:S(2)}, u32[]{:S(2)}) collective-permute-start(bf16[768,768]{1,0:T(8,128)(2,1)S(1)} %get-tuple-element.224.refs_1_), channel_id=1, source_target_pairs={{0,1},{1,0},{2,3},{3,2},{4,6},{5,7},{6,4},{7,5},{8,9},{9,8},{10,11... | collective-permute-start | bytes 3538952 | tf_op jit(solution)/shard_map/ppermute | solution.py:724
  183.0 13.1 %collective-permute-start.31 = (bf16[768,768]{1,0:T(8,128)(2,1)S(1)}, bf16[768,768]{1,0:T(8,128)(2,1)S(1)}, u32[]{:S(2)}, u32[]{:S(2)}) collective-permute-start(bf16[768,768]{1,0:T(8,128)(2,1)S(1)} %collective-permute-done.29.refs_2_), channel_id=1, source_target_pairs={{0,4},{4,0},{8,12},{12,8},{16,20},{20,16},{24,28},{28,24},{1,5},{5... | collective-permute-start | bytes 3538952 | tf_op jit(solution)/shard_map/ppermute | solution.py:605
  191.3 10.5 %collective-permute-start.28 = (bf16[192,768]{1,0:T(8,128)(2,1)S(1)}, bf16[192,768]{1,0:T(8,128)(2,1)S(1)}, u32[]{:S(2)}, u32[]{:S(2)}) collective-permute-start(bf16[192,768]{1,0:T(8,128)(2,1)S(1)} %get-tuple-element.219.refs_0_), channel_id=1, source_target_pairs={{0,8},{1,9},{2,10},{3,11},{4,20},{5,21},{6,22},{7,23},{8,0},{9,1},... | collective-permute-start | bytes 884744 | tf_op jit(solution)/shard_map/ppermute | solution.py:724
  212.0 16.3 %collective-permute-start.36 = (bf16[768,768]{1,0:T(8,128)(2,1)S(1)}, bf16[768,768]{1,0:T(8,128)(2,1)S(1)}, u32[]{:S(2)}, u32[]{:S(2)}) collective-permute-start(bf16[768,768]{1,0:T(8,128)(2,1)S(1)} %get-tuple-element.227.refs_1_), channel_id=1, source_target_pairs={{0,1},{1,0},{2,3},{3,2},{4,6},{5,7},{6,4},{7,5},{8,9},{9,8},{10,11... | collective-permute-start | bytes 3538952 | tf_op jit(solution)/shard_map/ppermute | solution.py:724
  (44 other events, 502.2 us)
where the time goes:
time: 235 us
  Pallas kernels  96.6 us (41%)
  waiting for transfers between devices  74.1 us (32%)
  starting transfers between devices  47.8 us (20%)
  local copies, waits for them, and re-layouts  13.7 us (6%)
    pallas_call x38, Pallas kernels, ordered(): pl.pallas_call(kernel, in_specs=list(in_specs) + [pl.BlockSpec(memory_spa...  96.6 us
    ppermute x26, waiting for transfers between devices, swap(): return lax.ppermute(value, ('batch', 'seq'), pairs)  68.9 us
    ppermute x26, starting transfers between devices, swap(): return lax.ppermute(value, ('batch', 'seq'), pairs)  39.4 us
    unnamed x66, local copies, waits for them, and re-layouts  10 us
    ppermute x13, starting transfers between devices, xor_permute(): return lax.ppermute(value, axis, [(i, i ^ mask) for i in range(size)])  8.32 us
    ppermute x13, waiting for transfers between devices, xor_permute(): return lax.ppermute(value, axis, [(i, i ^ mask) for i in range(size)])  5.15 us
  transfers between devices with their start and end apart: 39, of which 18 were waited for; matrix products, arithmetic and copies ran while one was open for 4% of the time, Pallas kernels for 31%

commit v1 on v0

--- a/solution.py
+++ b/solution.py
@@ -19,6 +19,7 @@
 F32 = jnp.float32
 VMEM_BYTES = 24 * 1024 * 1024
 EVENT_FLOPS = 50 * 10**6
+BACK_FLOPS = 5 * 10**7
 
 NN = (((1,), (0,)), ((), ()))
 NT = (((1,), (1,)), ((), ()))
@@ -178,30 +179,20 @@
 
 
 def feed_body(
-    info, o_in, x_in, cot_in, wo_any, wi_any, wu_any, vec,
+    info, o_in, x_in, cot_in, wo, wi, wu, vec,
     layer_out, u1_out, r1_out, g_second_out, g_outer_out, slope, small_out, hid_t, send,
-    wo, wi, wu, sems,
 ):
-    copies = [
-        pltpu.make_async_copy(src, dst, sems.at[i])
-        for i, (src, dst) in enumerate(((wo_any, wo), (wi_any, wi), (wu_any, wu)))
-    ]
-    for c in copies:
-        c.start()
     small_out[...] = jnp.zeros_like(small_out)
     width = wo.shape[0]
     chunks = wi.shape[1] // width
     b_out, fg, fs, b_outer, sg, ss = (vec[i : i + 1, :] for i in range(2, 8))
     att = o_in[...].astype(BF)
-    copies[0].wait()
     first_in = x_in[...].astype(F32) + (mm(att, wo[...]) + b_out)
     u1, r1 = norm_stats(first_in)
     u1_out[...] = u1
     r1_out[...] = jnp.broadcast_to(r1, r1_out.shape)
     first = u1 * fg + fs
     low = first.astype(BF)
-    copies[1].wait()
-    copies[2].wait()
     out = jnp.zeros_like(first)
     for j in range(chunks):
         cols = slice(j * width, (j + 1) * width)
@@ -239,7 +230,7 @@
     return ordered(
         feed_body,
         order,
-        [SM, VM, VM, VM, ANYWHERE, ANYWHERE, ANYWHERE, VM],
+        [SM] + [VM] * 7,
         (info, o, x, cot, wo, wi, wu, vec,),
         "feed",
         out_specs=[VM] * 9,
@@ -254,27 +245,15 @@
             jax.ShapeDtypeStruct((ff, tok), BF),
             pltpu.HBM((ff // 2, width), BF),
         ],
-        scratch_shapes=[
-            pltpu.VMEM((width, width), BF),
-            pltpu.VMEM((width, ff), BF),
-            pltpu.VMEM((ff, width), BF),
-            pltpu.SemaphoreType.DMA((3,)),
-        ],
         cost_estimate=cost(2 * tok * width * (5 * ff // 2 + width), 4 * (width * ff * 2), tok * ff),
         compiler_params=params(),
     )
 
 
 def inner_back_body(
-    info, u1_in, g_second_in, g_outer_in, slope, hid_t, wi_any, wu_any, vec,
+    info, u1_in, g_second_in, g_outer_in, slope, hid_t, wi, wu, vec,
     keep, g_in, low_t, back_out, small_out, send,
-    wi, wu, sems,
 ):
-    copies = [
-        pltpu.make_async_copy(src, dst, sems.at[i]) for i, (src, dst) in enumerate(((wu_any, wu), (wi_any, wi)))
-    ]
-    for c in copies:
-        c.start()
     small_out[...] = jnp.zeros_like(small_out)
     width = wi.shape[0]
     chunks = wi.shape[1] // width
@@ -286,8 +265,6 @@
     for c in range(2):
         put_pieces(low_t.at[c], 0, flat_t, info[2 + c])
     back = g_second_in[...]
-    copies[0].wait()
-    copies[1].wait()
     for j in range(chunks):
         cols = slice(j * width, (j + 1) * width)
         gi = (mm(g_outer, wu[cols, :], NT) * slope[:, cols]).astype(BF)
@@ -307,7 +284,7 @@
     return ordered(
         inner_back_body,
         order,
-        [SM] + [VM] * 5 + [ANYWHERE] * 2 + [VM],
+        [SM] + [VM] * 8,
         (info, u1, g_second, g_outer, slope, hid_t, wi, wu, vec,),
         "inner_back",
         out_specs=[VM] * 6,
@@ -318,11 +295,6 @@
             jax.ShapeDtypeStruct((tok, width), F32),
             jax.ShapeDtypeStruct((8, width), F32),
             half,
-        ],
-        scratch_shapes=[
-            pltpu.VMEM((width, ff), BF),
-            pltpu.VMEM((ff, width), BF),
-            pltpu.SemaphoreType.DMA((2,)),
         ],
         cost_estimate=cost(2 * tok * width * 3 * ff, 4 * (width * ff * 2)),
         compiler_params=params(),
@@ -436,7 +408,7 @@
         out_specs=[group(tok), group(total), group(total)],
         out_shape=[jax.ShapeDtypeStruct((groups, r, cols), BF) for r in (tok, total, total)],
         scratch_shapes=[pltpu.VMEM((cols, total), BF), pltpu.VMEM((cols, tok), F32)],
-        cost_estimate=cost(HEADS * 5 * 2 * tok * total * 256, 4 * total * width * 2, HEADS * tok * total),
+        cost_estimate=cost(BACK_FLOPS, 1 << 20),
         compiler_params=params(),
     )
 
@@ -609,6 +581,10 @@
     return pl.BlockSpec((count, 768), lambda *_: (index, 0))
 
 
+def in_hbm(array):
+    return pltpu.with_memory_space_constraint(array, pltpu.HBM) if array.shape[0] > 1024 else array
+
+
 def combine_body(ways, terms, extras, *refs):
     ins, outs = refs[: ways * terms + extras], refs[ways * terms + extras :]
     for w in range(ways):
@@ -630,7 +606,7 @@
         functools.partial(combine_body, len(ways), len(ways[0]), len(extras)),
         order,
         [rows_at(count, i) for _, i in terms] + [rows_at(32, i) for _, i in extras],
-        (*(a for a, _ in terms), *(a for a, _ in extras)),
+        (*(in_hbm(a) for a, _ in terms), *(in_hbm(a) for a, _ in extras)),
         "combine",
         grid=(1,),
         out_specs=[pl.BlockSpec(made.shape, lambda *_: (0, 0))] * len(ways),
@@ -659,7 +635,7 @@
         functools.partial(finish_body, len(arrays), len(extras)),
         order,
         [rows_at(count, 0)] * len(arrays) + [rows_at(32, i) for _, i in extras],
-        (*arrays, *(a for a, _ in extras)),
+        (*(in_hbm(a) for a in arrays), *(in_hbm(a) for a, _ in extras)),
         "finish",
         grid=(1,),
         out_specs=[pl.BlockSpec(o.shape, lambda *_: (0, 0)) for o in out],

time: 235 us -> 226 us (0.962)
  local copies, waits for them, and re-layouts: 13.7 us -> 9.3 us
  starting transfers between devices: 47.8 us -> 43.5 us
  waiting for transfers between devices: 74.1 us -> 70.7 us
  Pallas kernels: 96.6 us -> 99.1 us
    unnamed x66 -> x44, local copies, waits for them, and re-layouts: 10 us -> 5.63 us
    ppermute x26, starting transfers between devices: 39.4 us -> 35.3 us  [swap(): return lax.ppermute(value, ('batch', 'seq'), pairs)]
    ppermute x26, waiting for transfers between devices: 68.9 us -> 65.1 us  [swap(): return lax.ppermute(value, ('batch', 'seq'), pairs)]
    pallas_call x38, Pallas kernels: 96.6 us -> 99.1 us  [ordered(): pl.pallas_call(kernel, in_specs=list(in_specs) + [pl.BlockSpec(memory_spa...]
  transfers between devices with their start and end apart: 39 -> 39, of which waited for: 18 -> 17; matrix products, arithmetic and copies ran while one was open for 4% -> 4% of each run, Pallas kernels for 31% -> 34%
where the time goes in v1:
time: 226 us; the launch traced here: 225 us
  Pallas kernels  99.1 us (44%)
  waiting for transfers between devices  70.7 us (31%)
  starting transfers between devices  43.5 us (19%)
  local copies, waits for them, and re-layouts  9.3 us (4%)
    pallas_call x38, Pallas kernels, ordered(): pl.pallas_call(kernel, in_specs=list(in_specs) + [pl.BlockSpec(memory_spa...  99.1 us
    ppermute x26, waiting for transfers between devices, swap(): return lax.ppermute(value, ('batch', 'seq'), pairs)  65.1 us
    ppermute x26, starting transfers between devices, swap(): return lax.ppermute(value, ('batch', 'seq'), pairs)  35.3 us
    ppermute x13, starting transfers between devices, xor_permute(): return lax.ppermute(value, axis, [(i, i ^ mask) for i in range(size)])  8.2 us
    unnamed x44, local copies, waits for them, and re-layouts  5.63 us
    ppermute x13, waiting for transfers between devices, xor_permute(): return lax.ppermute(value, axis, [(i, i ^ mask) for i in range(size)])  5.59 us
  transfers between devices with their start and end apart: 39, of which 17 were waited for; matrix products, arithmetic and copies ran while one was open for 4% of the time, Pallas kernels for 34%

profile of v1, /device:TPU:0, one launch (start us, length us, event | category | flops | bytes accessed | tf_op | source)
XLA Modules:
  0.0 224.9 jit_solution(11442466659774009013)
XLA Ops:
  0.7 3.0 %collective-permute-start.1 = (bf16[256,768]{1,0:T(8,128)(2,1)}, bf16[256,768]{1,0:T(8,128)(2,1)S(1)}, u32[]{:S(2)}, u32[]{:S(2)}) collective-permute-start(bf16[256,768]{1,0:T(8,128)(2,1)} %bitcast.20), channel_id=1, source_target_pairs={{0,2},{1,3},{2,0},{3,1},{4,6},{5,7},{6,4},{7,5},{8,10},{9,11},{10,... | collective-permute-start | bytes 1179656 | tf_op jit(solution)/shard_map/ppermute | solution.py:577
  20.6 12.4 %attend.1 = (bf16[256,768]{1,0:T(8,128)(2,1)}, bf16[3,1024,256]{2,1,0:T(8,128)(2,1)}, bf16[3,1024,256]{2,1,0:T(8,128)(2,1)}, f32[256,768]{1,0:T(8,128)S(1)}, f32...) custom-call(bf16[256,768]{1,0:T(8,128)(2,1)S(1)} %bitcast.22, bf16[256,768]{1,0:T(8,128)(2,1)S(1)} %collective-permute-done.refs_1_.refs_9_, ...), custom_call_target="tpu_custom_call" | custom-call | flops 563714457600 | bytes 629145600 | tf_op jit(solution)/shard_map/attend/pallas_call | solution.py:58
  33.1 8.4 %feed.1 = (bf16[256,768]{1,0:T(8,128)(2,1)}, f32[256,768]{1,0:T(8,128)S(1)}, f32[256,128]{1,0:T(8,128)S(1)}, f32[256,768]{1,0:T(8,128)S(1)}, bf16[256,768]{1,0:T...) custom-call(s32[7]{0:T(128)S(1)} %stack.40.refs_0_, ...), custom_call_target="tpu_custom_call" | custom-call | flops 332188876800 | bytes 1887436800 | tf_op jit(solution)/shard_map/feed/pallas_call | solution.py:58
  41.5 6.7 %inner_back.1 = (bf16[1536,768]{1,0:T(8,128)(2,1)}, bf16[256,3072]{1,0:T(8,128)(2,1)S(1)}, bf16[2,768,256]{2,1,0:T(8,128)(2,1)S(1)}, f32[256,768]{1,0:T(8,128)S(...) custom-call(s32[7]{0:T(128)S(1)} %stack.40.refs_0_, ...), custom_call_target="tpu_custom_call" | custom-call | flops 362387865600 | bytes 1887436800 | tf_op jit(solution)/shard_map/inner_back/pallas_call | solution.py:58
  48.7 3.0 %combine.13 = (bf16[768,768]{1,0:T(8,128)(2,1)}, f32[8,128]{1,0:T(8,128)S(1)}) custom-call(bf16[1536,768]{1,0:T(8,128)(2,1)} %get-tuple-element.147.refs_0_, bf16[1536,768]{1,0:T(8,128)(2,1)} %collective-permute-done.4.refs_1_, f32[8,128]{1,0:T(8,128)S(1)} %get-tuple-element.149.refs_2_), custom_call_target="tpu_custom_call" | custom-call | flops 5000000000 | bytes 104857600 | tf_op jit(solution)/shard_map/combine/pallas_call | solution.py:58
  52.9 4.4 %branch_back.1 = (bf16[1536,768]{1,0:T(8,128)(2,1)}, f32[256,768]{1,0:T(8,128)}, bf16[256,768]{1,0:T(8,128)(2,1)}, f32[16,256]{1,0:T(8,128)S(1)}, f32[8,768]{1,0...) custom-call(s32[7]{0:T(128)S(1)} %stack.40.refs_0_, f32[256,768]{1,0:T(8,128)S(1)} %copy-done.17, ...), custom_call_target="tpu_custom_call" | custom-call | flops 120795955200 | bytes 943718400 | tf_op jit(solution)/shard_map/branch_back/pallas_call | solution.py:58
  57.3 2.9 %combine.14 = (bf16[768,768]{1,0:T(8,128)(2,1)}, f32[8,128]{1,0:T(8,128)S(1)}) custom-call(bf16[1536,768]{1,0:T(8,128)(2,1)} %get-tuple-element.158.refs_0_, bf16[1536,768]{1,0:T(8,128)(2,1)} %collective-permute-done.5.refs_1_, f32[8,128]{1,0:T(8,128)S(1)} %get-tuple-element.160.refs_2_), custom_call_target="tpu_custom_call" | custom-call | flops 5000000000 | bytes 104857600 | tf_op jit(solution)/shard_map/combine/pallas_call | solution.py:58
  61.1 12.8 %attend_back.1 = (bf16[3,256,256]{2,1,0:T(8,128)(2,1)S(1)}, bf16[3,1024,256]{2,1,0:T(8,128)(2,1)S(1)}, bf16[3,1024,256]{2,1,0:T(8,128)(2,1)S(1)}, f32[8,128]{1,0:T(8,128)S(1)}) custom-call(bf16[256,768]{1,0:T(8,128)(2,1)} %get-tuple-element.152.refs_0_, bf16[3,1024,256]{2,1,0:T(8,128)(2,1)} %get-tuple-element.153.refs_1_, ...), custom_call_target="tpu_custom_call" | custom-call | flops 5000000000 | bytes 104857600 | tf_op jit(solution)/shard_map/attend_back/pallas_call | solution.py:58
  78.0 6.7 %weights.1 = (bf16[1568,768]{1,0:T(8,128)(2,1)}, bf16[1568,768]{1,0:T(8,128)(2,1)}, f32[8,128]{1,0:T(8,128)S(1)}) custom-call(s32[7]{0:T(128)S(1)} %stack.40.refs_0_, bf16[768,768]{1,0:T(8,128)(2,1)S(1)} %copy-done.14, f32[8,768]{1,0:T(8,128)S(1)} %get-tuple-element.170.refs_2_, f32[8,768]{1,0:T(8,128)S(1)} %get-tuple-element.171.refs_3_, ...), custom_call_target="tpu_custom_call" | custom-call | flops 271790899200 | bytes 943718400 | tf_op jit(solution)/shard_map/weights/pallas_call | solution.py:58
  91.5 3.5 %token_parts.1 = (f32[256,768]{1,0:T(8,128)S(1)}, bf16[512,768]{1,0:T(8,128)(2,1)S(1)}, bf16[256,768]{1,0:T(8,128)(2,1)S(1)}, f32[8,128]{1,0:T(8,128)S(1)}) custom-call(s32[7]{0:T(128)S(1)} %stack.40.refs_0_, bf16[768,768]{1,0:T(8,128)(2,1)S(1)} %copy-done.4, bf16[768,768]{1,0:T(8,128)(2,1)S(1)} %copy-done.5, bf16[768,768]{1,0:T(8,128)(2,1)S(1)} %copy-done.6, ...), custom_call_target="tpu_custom_call" | custom-call | flops 271790899200 | bytes 943718400 | tf_op jit(solution)/shard_map/token_parts/pallas_call | solution.py:58
  106.7 4.0 %collective-permute-done.13.refs_4_ = bf16[192,768]{1,0:T(8,128)(2,1)S(1)} collective-permute-done((bf16[192,768]{1,0:T(8,128)(2,1)S(1)}, bf16[192,768]{1,0:T(8,128)(2,1)S(1)}, u32[]{:S(2)}, u32[]{:S(2)}) %collective-permute-start.13) | collective-permute-done | bytes 294944 | tf_op jit(solution)/shard_map/ppermute | solution.py:700
  113.2 2.9 %collective-permute-start.17 = (bf16[96,768]{1,0:T(8,128)(2,1)S(1)}, bf16[96,768]{1,0:T(8,128)(2,1)S(1)}, u32[]{:S(2)}, u32[]{:S(2)}) collective-permute-start(bf16[96,768]{1,0:T(8,128)(2,1)S(1)} %get-tuple-element.194.refs_0_), channel_id=1, source_target_pairs={{0,16},{1,17},{2,18},{3,19},{4,12},{5,13},{6,14},{7,15},{8,24},{9,... | collective-permute-start | bytes 442376 | tf_op jit(solution)/shard_map/ppermute | solution.py:700
  118.3 6.7 %collective-permute-done.18.refs_5_ = bf16[96,768]{1,0:T(8,128)(2,1)S(1)} collective-permute-done((bf16[96,768]{1,0:T(8,128)(2,1)S(1)}, bf16[96,768]{1,0:T(8,128)(2,1)S(1)}, u32[]{:S(2)}, u32[]{:S(2)}) %collective-permute-start.18) | collective-permute-done | bytes 147488 | tf_op jit(solution)/shard_map/ppermute | solution.py:700
  126.4 3.5 %collective-permute-start.20 = (bf16[192,768]{1,0:T(8,128)(2,1)S(1)}, bf16[192,768]{1,0:T(8,128)(2,1)S(1)}, u32[]{:S(2)}, u32[]{:S(2)}) collective-permute-start(bf16[192,768]{1,0:T(8,128)(2,1)S(1)} %get-tuple-element.202.refs_0_), channel_id=1, source_target_pairs={{0,8},{1,9},{2,10},{3,11},{4,20},{5,21},{6,22},{7,23},{8,0},{9,1},... | collective-permute-start | bytes 884744 | tf_op jit(solution)/shard_map/ppermute | solution.py:700
  129.9 5.0 %collective-permute-done.16.refs_2_.refs_4_ = bf16[800,768]{1,0:T(8,128)(2,1)S(1)} collective-permute-done((bf16[800,768]{1,0:T(8,128)(2,1)S(1)}, bf16[800,768]{1,0:T(8,128)(2,1)S(1)}, u32[]{:S(2)}, u32[]{:S(2)}) %collective-permute-start.16) | collective-permute-done | bytes 1228832 | tf_op jit(solution)/shard_map/ppermute | solution.py:700
  140.2 6.7 %collective-permute-done.19.refs_3_.refs_5_ = bf16[416,768]{1,0:T(8,128)(2,1)S(1)} collective-permute-done((bf16[416,768]{1,0:T(8,128)(2,1)S(1)}, bf16[416,768]{1,0:T(8,128)(2,1)S(1)}, u32[]{:S(2)}, u32[]{:S(2)}) %collective-permute-start.19) | collective-permute-done | bytes 639008 | tf_op jit(solution)/shard_map/ppermute | solution.py:700
  148.7 4.5 %collective-permute-done.23.refs_1_ = bf16[384,768]{1,0:T(8,128)(2,1)S(1)} collective-permute-done((bf16[384,768]{1,0:T(8,128)(2,1)S(1)}, bf16[384,768]{1,0:T(8,128)(2,1)S(1)}, u32[]{:S(2)}, u32[]{:S(2)}) %collective-permute-start.23) | collective-permute-done | bytes 589856 | tf_op jit(solution)/shard_map/ppermute | solution.py:700
  161.5 8.7 %collective-permute-done.26.refs_1_ = bf16[384,768]{1,0:T(8,128)(2,1)S(1)} collective-permute-done((bf16[384,768]{1,0:T(8,128)(2,1)S(1)}, bf16[384,768]{1,0:T(8,128)(2,1)S(1)}, u32[]{:S(2)}, u32[]{:S(2)}) %collective-permute-start.26) | collective-permute-done | bytes 589856 | tf_op jit(solution)/shard_map/ppermute | solution.py:700
  175.1 2.9 %collective-permute-start.27 = (bf16[96,768]{1,0:T(8,128)(2,1)S(1)}, bf16[96,768]{1,0:T(8,128)(2,1)S(1)}, u32[]{:S(2)}, u32[]{:S(2)}) collective-permute-start(bf16[96,768]{1,0:T(8,128)(2,1)S(1)} %get-tuple-element.217.refs_0_), channel_id=1, source_target_pairs={{0,16},{1,17},{2,18},{3,19},{4,12},{5,13},{6,14},{7,15},{8,24},{9,... | collective-permute-start | bytes 442376 | tf_op jit(solution)/shard_map/ppermute | solution.py:700
  178.0 3.8 %collective-permute-done.27.refs_1_ = bf16[96,768]{1,0:T(8,128)(2,1)S(1)} collective-permute-done((bf16[96,768]{1,0:T(8,128)(2,1)S(1)}, bf16[96,768]{1,0:T(8,128)(2,1)S(1)}, u32[]{:S(2)}, u32[]{:S(2)}) %collective-permute-start.27) | collective-permute-done | bytes 147488 | tf_op jit(solution)/shard_map/ppermute | solution.py:700
  186.6 4.4 %unpack_rows.1 = (f32[3072,768]{1,0:T(8,128)}, f32[8,128]{1,0:T(8,128)S(1)}) custom-call(s32[7]{0:T(128)S(1)} %stack.40.refs_0_, bf16[768,768]{1,0:T(8,128)(2,1)S(1)} %get-tuple-element.220.refs_1_, bf16[768,768]{1,0:T(8,128)(2,1)S(1)} %collective-permute-done.29.refs_2_, bf16[768,768]{1,0:T(8,128)(2,1)S(1)} %collective-permute-done.30.refs_3_, ...), custom_call_target="tpu_custom_call" | custom-call | flops 235929600 | bytes 1415577600 | tf_op jit(solution)/shard_map/unpack_rows/pallas_call | solution.py:58
  193.3 4.4 %unpack_cols.1 = (f32[768,3072]{1,0:T(8,128)}, f32[8,128]{1,0:T(8,128)S(1)}) custom-call(s32[7]{0:T(128)S(1)} %stack.40.refs_0_, bf16[768,768]{1,0:T(8,128)(2,1)S(1)} %get-tuple-element.224.refs_1_, bf16[768,768]{1,0:T(8,128)(2,1)S(1)} %collective-permute-done.33.refs_2_, bf16[768,768]{1,0:T(8,128)(2,1)S(1)} %collective-permute-done.34.refs_3_, ...), custom_call_target="tpu_custom_call" | custom-call | flops 235929600 | bytes 1415577600 | tf_op jit(solution)/shard_map/unpack_cols/pallas_call | solution.py:58
  197.7 4.5 %collective-permute-done.32.refs_1_ = bf16[384,768]{1,0:T(8,128)(2,1)S(1)} collective-permute-done((bf16[384,768]{1,0:T(8,128)(2,1)S(1)}, bf16[384,768]{1,0:T(8,128)(2,1)S(1)}, u32[]{:S(2)}, u32[]{:S(2)}) %collective-permute-start.32) | collective-permute-done | bytes 589856 | tf_op jit(solution)/shard_map/ppermute | solution.py:700
  208.1 10.5 %collective-permute-done.36.refs_1_ = bf16[768,768]{1,0:T(8,128)(2,1)S(1)} collective-permute-done((bf16[768,768]{1,0:T(8,128)(2,1)S(1)}, bf16[768,768]{1,0:T(8,128)(2,1)S(1)}, u32[]{:S(2)}, u32[]{:S(2)}) %collective-permute-start.36) | collective-permute-done | bytes 1179680 | tf_op jit(solution)/shard_map/ppermute | solution.py:700
  (159 shorter events, 86.5 us)
Async XLA Ops:
  0.7 12.6 %collective-permute-start.1 = (bf16[256,768]{1,0:T(8,128)(2,1)}, bf16[256,768]{1,0:T(8,128)(2,1)S(1)}, u32[]{:S(2)}, u32[]{:S(2)}) collective-permute-start(bf16[256,768]{1,0:T(8,128)(2,1)} %bitcast.20), channel_id=1, source_target_pairs={{0,2},{1,3},{2,0},{3,1},{4,6},{5,7},{6,4},{7,5},{8,10},{9,11},{10,... | collective-permute-start | bytes 1179656 | tf_op jit(solution)/shard_map/ppermute | solution.py:577
  3.7 11.1 %collective-permute-start = (bf16[256,768]{1,0:T(8,128)(2,1)}, bf16[256,768]{1,0:T(8,128)(2,1)S(1)}, u32[]{:S(2)}, u32[]{:S(2)}) collective-permute-start(bf16[256,768]{1,0:T(8,128)(2,1)} %bitcast.21), channel_id=1, source_target_pairs={{0,1},{1,0},{2,3},{3,2},{4,5},{5,4},{6,7},{7,6},{8,9},{9,8},{10,11... | collective-permute-start | bytes 1179656 | tf_op jit(solution)/shard_map/ppermute | solution.py:577
  51.8 22.2 %collective-permute-start.6 = (bf16[768,768]{1,0:T(8,128)(2,1)}, bf16[768,768]{1,0:T(8,128)(2,1)S(1)}, u32[]{:S(2)}, u32[]{:S(2)}) collective-permute-start(bf16[768,768]{1,0:T(8,128)(2,1)} %get-tuple-element.165), channel_id=1, source_target_pairs={{0,1},{1,0},{2,3},{3,2},{4,6},{5,7},{6,4},{7,5},{8,9},{9,8},{10,11... | collective-permute-start | bytes 3538952 | tf_op jit(solution)/shard_map/ppermute | solution.py:700
  60.3 24.5 %collective-permute-start.8 = (bf16[768,768]{1,0:T(8,128)(2,1)}, bf16[768,768]{1,0:T(8,128)(2,1)}, u32[]{:S(2)}, u32[]{:S(2)}) collective-permute-start(bf16[768,768]{1,0:T(8,128)(2,1)} %get-tuple-element.168), channel_id=1, source_target_pairs={{0,1},{1,0},{2,3},{3,2},{4,6},{5,7},{6,4},{7,5},{8,9},{9,8},{10,11... | collective-permute-start | bytes 3538952 | tf_op jit(solution)/shard_map/ppermute | solution.py:700
  76.4 11.2 %collective-permute-start.7 = (bf16[384,768]{1,0:T(8,128)(2,1)}, bf16[384,768]{1,0:T(8,128)(2,1)}, u32[]{:S(2)}, u32[]{:S(2)}) collective-permute-start(bf16[384,768]{1,0:T(8,128)(2,1)} %get-tuple-element.167), channel_id=1, source_target_pairs={{0,2},{1,3},{2,0},{3,1},{4,5},{5,4},{6,7},{7,6},{8,10},{9,11},{10,... | collective-permute-start | bytes 1769480 | tf_op jit(solution)/shard_map/ppermute | solution.py:700
  87.7 17.1 %collective-permute-start.14 = (bf16[1568,768]{1,0:T(8,128)(2,1)}, bf16[1568,768]{1,0:T(8,128)(2,1)}, u32[]{:S(2)}, u32[]{:S(2)}) collective-permute-start(bf16[1568,768]{1,0:T(8,128)(2,1)} %get-tuple-element.187), channel_id=1, source_target_pairs={{0,4},{4,0},{8,12},{12,8},{16,20},{20,16},{24,28},{28,24},{1,5},{5... | collective-permute-start | bytes 7225352 | tf_op jit(solution)/shard_map/ppermute | solution.py:577
  89.9 11.0 %collective-permute-start.10 = (bf16[192,768]{1,0:T(8,128)(2,1)}, bf16[192,768]{1,0:T(8,128)(2,1)}, u32[]{:S(2)}, u32[]{:S(2)}) collective-permute-start(bf16[192,768]{1,0:T(8,128)(2,1)} %get-tuple-element.180), channel_id=1, source_target_pairs={{0,8},{1,9},{2,10},{3,11},{4,20},{5,21},{6,22},{7,23},{8,0},{9,1},... | collective-permute-start | bytes 884744 | tf_op jit(solution)/shard_map/ppermute | solution.py:700
  98.7 12.0 %collective-permute-start.13 = (bf16[192,768]{1,0:T(8,128)(2,1)S(1)}, bf16[192,768]{1,0:T(8,128)(2,1)S(1)}, u32[]{:S(2)}, u32[]{:S(2)}) collective-permute-start(bf16[192,768]{1,0:T(8,128)(2,1)S(1)} %get-tuple-element.185), channel_id=1, source_target_pairs={{0,8},{1,9},{2,10},{3,11},{4,20},{5,21},{6,22},{7,23},{8,0},{9,1},... | collective-permute-start | bytes 884744 | tf_op jit(solution)/shard_map/ppermute | solution.py:700
  100.4 16.7 %collective-permute-start.9 = (bf16[512,768]{1,0:T(8,128)(2,1)S(1)}, bf16[512,768]{1,0:T(8,128)(2,1)S(1)}, u32[]{:S(2)}, u32[]{:S(2)}) collective-permute-start(bf16[512,768]{1,0:T(8,128)(2,1)S(1)} %get-tuple-element.178), channel_id=1, source_target_pairs={{0,1},{1,0},{2,3},{3,2},{4,6},{5,7},{6,4},{7,5},{8,9},{9,8},{10,11... | collective-permute-start | bytes 2359304 | tf_op jit(solution)/shard_map/ppermute | solution.py:700
  113.2 13.1 %collective-permute-start.17 = (bf16[96,768]{1,0:T(8,128)(2,1)S(1)}, bf16[96,768]{1,0:T(8,128)(2,1)S(1)}, u32[]{:S(2)}, u32[]{:S(2)}) collective-permute-start(bf16[96,768]{1,0:T(8,128)(2,1)S(1)} %get-tuple-element.194.refs_0_), channel_id=1, source_target_pairs={{0,16},{1,17},{2,18},{3,19},{4,12},{5,13},{6,14},{7,15},{8,24},{9,... | collective-permute-start | bytes 442376 | tf_op jit(solution)/shard_map/ppermute | solution.py:700
  116.2 18.7 %collective-permute-start.16 = (bf16[800,768]{1,0:T(8,128)(2,1)S(1)}, bf16[800,768]{1,0:T(8,128)(2,1)S(1)}, u32[]{:S(2)}, u32[]{:S(2)}) collective-permute-start(bf16[800,768]{1,0:T(8,128)(2,1)S(1)} %get-tuple-element.193.refs_3_), channel_id=1, source_target_pairs={{0,1},{1,0},{2,3},{3,2},{4,6},{5,7},{6,4},{7,5},{8,9},{9,8},{10,11... | collective-permute-start | bytes 3686408 | tf_op jit(solution)/shard_map/ppermute | solution.py:700
  117.2 19.8 %collective-permute-start.15 = (bf16[256,768]{1,0:T(8,128)(2,1)S(1)}, bf16[256,768]{1,0:T(8,128)(2,1)S(1)}, u32[]{:S(2)}, u32[]{:S(2)}) collective-permute-start(bf16[256,768]{1,0:T(8,128)(2,1)S(1)} %get-tuple-element.192), channel_id=1, source_target_pairs={{0,2},{1,3},{2,0},{3,1},{4,5},{5,4},{6,7},{7,6},{8,10},{9,11},{10,... | collective-permute-start | bytes 1179656 | tf_op jit(solution)/shard_map/ppermute | solution.py:700
  126.3 11.7 %collective-permute-start.21 = (bf16[96,768]{1,0:T(8,128)(2,1)S(1)}, bf16[96,768]{1,0:T(8,128)(2,1)S(1)}, u32[]{:S(2)}, u32[]{:S(2)}) collective-permute-start(bf16[96,768]{1,0:T(8,128)(2,1)S(1)} %get-tuple-element.203.refs_0_), channel_id=1, source_target_pairs={{0,16},{1,17},{2,18},{3,19},{4,12},{5,13},{6,14},{7,15},{8,24},{9,... | collective-permute-start | bytes 442376 | tf_op jit(solution)/shard_map/ppermute | solution.py:700
  126.4 12.3 %collective-permute-start.20 = (bf16[192,768]{1,0:T(8,128)(2,1)S(1)}, bf16[192,768]{1,0:T(8,128)(2,1)S(1)}, u32[]{:S(2)}, u32[]{:S(2)}) collective-permute-start(bf16[192,768]{1,0:T(8,128)(2,1)S(1)} %get-tuple-element.202.refs_0_), channel_id=1, source_target_pairs={{0,8},{1,9},{2,10},{3,11},{4,20},{5,21},{6,22},{7,23},{8,0},{9,1},... | collective-permute-start | bytes 884744 | tf_op jit(solution)/shard_map/ppermute | solution.py:700
  136.4 10.5 %collective-permute-start.19 = (bf16[416,768]{1,0:T(8,128)(2,1)S(1)}, bf16[416,768]{1,0:T(8,128)(2,1)S(1)}, u32[]{:S(2)}, u32[]{:S(2)}) collective-permute-start(bf16[416,768]{1,0:T(8,128)(2,1)S(1)} %get-tuple-element.201.refs_4_), channel_id=1, source_target_pairs={{0,2},{1,3},{2,0},{3,1},{4,5},{5,4},{6,7},{7,6},{8,10},{9,11},{10,... | collective-permute-start | bytes 1916936 | tf_op jit(solution)/shard_map/ppermute | solution.py:700
  138.0 10.7 %collective-permute-start.24 = (bf16[192,768]{1,0:T(8,128)(2,1)S(1)}, bf16[192,768]{1,0:T(8,128)(2,1)S(1)}, u32[]{:S(2)}, u32[]{:S(2)}) collective-permute-start(bf16[192,768]{1,0:T(8,128)(2,1)S(1)} %get-tuple-element.209.refs_0_), channel_id=1, source_target_pairs={{0,8},{1,9},{2,10},{3,11},{4,20},{5,21},{6,22},{7,23},{8,0},{9,1},... | collective-permute-start | bytes 884744 | tf_op jit(solution)/shard_map/ppermute | solution.py:700
  138.7 14.4 %collective-permute-start.23 = (bf16[384,768]{1,0:T(8,128)(2,1)S(1)}, bf16[384,768]{1,0:T(8,128)(2,1)S(1)}, u32[]{:S(2)}, u32[]{:S(2)}) collective-permute-start(bf16[384,768]{1,0:T(8,128)(2,1)S(1)} %get-tuple-element.208.refs_0_), channel_id=1, source_target_pairs={{0,2},{1,3},{2,0},{3,1},{4,5},{5,4},{6,7},{7,6},{8,10},{9,11},{10,... | collective-permute-start | bytes 1769480 | tf_op jit(solution)/shard_map/ppermute | solution.py:700
  153.2 20.7 %collective-permute-start.29 = (bf16[768,768]{1,0:T(8,128)(2,1)S(1)}, bf16[768,768]{1,0:T(8,128)(2,1)S(1)}, u32[]{:S(2)}, u32[]{:S(2)}) collective-permute-start(bf16[768,768]{1,0:T(8,128)(2,1)S(1)} %get-tuple-element.220.refs_1_), channel_id=1, source_target_pairs={{0,1},{1,0},{2,3},{3,2},{4,6},{5,7},{6,4},{7,5},{8,9},{9,8},{10,11... | collective-permute-start | bytes 3538952 | tf_op jit(solution)/shard_map/ppermute | solution.py:700
  153.8 16.3 %collective-permute-start.26 = (bf16[384,768]{1,0:T(8,128)(2,1)S(1)}, bf16[384,768]{1,0:T(8,128)(2,1)S(1)}, u32[]{:S(2)}, u32[]{:S(2)}) collective-permute-start(bf16[384,768]{1,0:T(8,128)(2,1)S(1)} %get-tuple-element.214.refs_0_), channel_id=1, source_target_pairs={{0,2},{1,3},{2,0},{3,1},{4,5},{5,4},{6,7},{7,6},{8,10},{9,11},{10,... | collective-permute-start | bytes 1769480 | tf_op jit(solution)/shard_map/ppermute | solution.py:700
  155.0 31.6 %collective-permute-start.30 = (bf16[768,768]{1,0:T(8,128)(2,1)S(1)}, bf16[768,768]{1,0:T(8,128)(2,1)S(1)}, u32[]{:S(2)}, u32[]{:S(2)}) collective-permute-start(bf16[768,768]{1,0:T(8,128)(2,1)S(1)} %get-tuple-element.220.refs_1_), channel_id=1, source_target_pairs={{0,4},{4,0},{8,12},{12,8},{16,20},{20,16},{24,28},{28,24},{1,5},{5... | collective-permute-start | bytes 3538952 | tf_op jit(solution)/shard_map/ppermute | solution.py:577
  158.9 15.0 %collective-permute-start.25 = (bf16[128,768]{1,0:T(8,128)(2,1)S(1)}, bf16[128,768]{1,0:T(8,128)(2,1)S(1)}, u32[]{:S(2)}, u32[]{:S(2)}) collective-permute-start(bf16[128,768]{1,0:T(8,128)(2,1)S(1)} %get-tuple-element.213.refs_6_), channel_id=1, source_target_pairs={{0,16},{1,17},{2,18},{3,19},{4,12},{5,13},{6,14},{7,15},{8,24},{9,... | collective-permute-start | bytes 589832 | tf_op jit(solution)/shard_map/ppermute | solution.py:700
  170.2 16.4 %collective-permute-start.33 = (bf16[768,768]{1,0:T(8,128)(2,1)S(1)}, bf16[768,768]{1,0:T(8,128)(2,1)S(1)}, u32[]{:S(2)}, u32[]{:S(2)}) collective-permute-start(bf16[768,768]{1,0:T(8,128)(2,1)S(1)} %get-tuple-element.224.refs_1_), channel_id=1, source_target_pairs={{0,1},{1,0},{2,3},{3,2},{4,6},{5,7},{6,4},{7,5},{8,9},{9,8},{10,11... | collective-permute-start | bytes 3538952 | tf_op jit(solution)/shard_map/ppermute | solution.py:700
  174.0 12.6 %collective-permute-start.31 = (bf16[768,768]{1,0:T(8,128)(2,1)S(1)}, bf16[768,768]{1,0:T(8,128)(2,1)S(1)}, u32[]{:S(2)}, u32[]{:S(2)}) collective-permute-start(bf16[768,768]{1,0:T(8,128)(2,1)S(1)} %collective-permute-done.29.refs_2_), channel_id=1, source_target_pairs={{0,4},{4,0},{8,12},{12,8},{16,20},{20,16},{24,28},{28,24},{1,5},{5... | collective-permute-start | bytes 3538952 | tf_op jit(solution)/shard_map/ppermute | solution.py:577
  202.3 16.3 %collective-permute-start.36 = (bf16[768,768]{1,0:T(8,128)(2,1)S(1)}, bf16[768,768]{1,0:T(8,128)(2,1)S(1)}, u32[]{:S(2)}, u32[]{:S(2)}) collective-permute-start(bf16[768,768]{1,0:T(8,128)(2,1)S(1)} %get-tuple-element.227.refs_1_), channel_id=1, source_target_pairs={{0,1},{1,0},{2,3},{3,2},{4,6},{5,7},{6,4},{7,5},{8,9},{9,8},{10,11... | collective-permute-start | bytes 3538952 | tf_op jit(solution)/shard_map/ppermute | solution.py:700
  (33 other events, 259.4 us)

commit v2 on v1

--- a/solution.py
+++ b/solution.py
@@ -18,7 +18,7 @@
 BF = jnp.bfloat16
 F32 = jnp.float32
 VMEM_BYTES = 24 * 1024 * 1024
-EVENT_FLOPS = 50 * 10**6
+EVENT_FLOPS = 43 * 10**6
 BACK_FLOPS = 5 * 10**7
 
 NN = (((1,), (0,)), ((), ()))
@@ -90,7 +90,7 @@
         k_out[0, start : start + count, :] = mm(x, wk[...]).astype(BF)
         v = mm(x, wv[...]) + vec[1:2, :]
         v_out[0, start : start + count, :] = v.astype(BF)
-        vt[:, start : start + count] = v.T.astype(BF)
+        vt[:, start : start + count] = v.astype(BF).T
         start += count
     total = start
     step = 256
@@ -203,7 +203,7 @@
             0.7978845608028654 * (1.0 + 3.0 * 0.044715 * v * v)
         )
         out = out + mm(h.astype(BF), wu[cols, :])
-        put_pieces(hid_t, j * width, h.T.astype(BF), info[2 + 2 * j // chunks])
+        put_pieces(hid_t, j * width, h.astype(BF).T, info[2 + 2 * j // chunks])
     u2, r2 = norm_stats(first + (out + b_outer))
     layer_out[...] = (u2 * sg + ss).astype(BF)
     cot = cot_in[...].astype(F32)
@@ -261,7 +261,7 @@
     for j in range(chunks // 2):
         at = pl.multiple_of((j ^ info[0]) * width, width)
         keep[j * width : (j + 1) * width, :] = mm(hid_t[pl.ds(at, width), :], g_outer).astype(BF)
-    flat_t = (u1_in[...] * vec[3:4, :] + vec[4:5, :]).T.astype(BF)
+    flat_t = (u1_in[...] * vec[3:4, :] + vec[4:5, :]).astype(BF).T
     for c in range(2):
         put_pieces(low_t.at[c], 0, flat_t, info[2 + c])
     back = g_second_in[...]
@@ -321,7 +321,7 @@
     o = o_in[...]
     g_att = mm(g_branch, wo_in[...], NT).astype(BF)
     g_att_out[...] = g_att
-    put_pieces(att_t, 0, o.T.astype(BF), info[2])
+    put_pieces(att_t, 0, o.astype(BF).T, info[2])
     wo_a[...] = mm(att_t[...], g_branch).astype(BF)
     head = lax.broadcasted_iota(jnp.int32, (16, width), 0)
     lane = lax.broadcasted_iota(jnp.int32, (16, width), 1)
@@ -359,7 +359,7 @@
     total = k_in.shape[1]
     step = 256
     per = step // BLK
-    kt[...] = k_in[0].astype(F32).T.astype(BF)
+    kt[...] = k_in[0].T
     for pair in range(QUAD // 2):
         lanes = slice(pair * 128, pair * 128 + 128)
         qs = [half_mask(q_in[:, lanes], s) for s in range(2)]
@@ -424,7 +424,7 @@
     own = rows[0]
     start = 0
     for piece, count in zip(pieces, rows):
-        t = piece[...].astype(F32).T.astype(BF)
+        t = piece[...].T
         for p in range(t.shape[0] // 96):
             for xt, mix in ((x0, info[2]), (x1, info[3])):
                 if start < own or xt is x1:
@@ -524,31 +524,33 @@
     count = len(refs) - 2
     outs, wide, sems = refs[:count], refs[count], refs[count + 1]
     size = 96
-    width = ins[0].shape[1]
-    places = []
-    for b, (ref, (side, j)) in enumerate(zip(ins, blocks)):
-        for i in range(width // size):
-            at = pl.multiple_of((i ^ info[5 + side]) * size, 32)
+    rows, width = ins[0].shape
+    pieces = rows // size
+    copies = []
+    for b, (ref, (side, j, half)) in enumerate(zip(ins, blocks)):
+        mix = info[5 + side]
+        for i in range(pieces):
+            at = pl.multiple_of((i ^ (mix & (pieces - 1))) * size, 32)
             wide[b, pl.ds(at, size), :] = ref[i * size : (i + 1) * size, :].astype(F32)
         chunk = info[side] ^ j
         if kind == "four":
-            places.append([(chunk == c, outs[c]) for c in range(4)])
+            at = pl.multiple_of((half ^ (mix // pieces)) * rows, rows)
+            targets = [(chunk == c, outs[c].at[pl.ds(at, rows), :]) for c in range(4)]
         else:
             at = pl.multiple_of(chunk * width, width)
-            places.append([(None, outs[0].at[pl.ds(at, width), :] if kind == "rows" else outs[0].at[:, pl.ds(at, width)])])
-        for when, out in places[b]:
+            targets = [(None, outs[0].at[pl.ds(at, width), :] if kind == "rows" else outs[0].at[:, pl.ds(at, width)])]
+        for when, out in targets:
             copy = pltpu.make_async_copy(wide.at[b], out, sems.at[b])
+            copies.append((when, copy))
             if when is None:
                 copy.start()
             else:
                 pl.when(when)(copy.start)
-    for b in range(n):
-        for when, out in places[b]:
-            copy = pltpu.make_async_copy(wide.at[b], out, sems.at[b])
-            if when is None:
-                copy.wait()
-            else:
-                pl.when(when)(copy.wait)
+    for when, copy in copies:
+        if when is None:
+            copy.wait()
+        else:
+            pl.when(when)(copy.wait)
 
 
 def unpack(order, kind, info, arrays, blocks, width, ff, made=()):
@@ -565,7 +567,10 @@
         "unpack_" + kind,
         out_specs=[ANYWHERE] * len(shapes),
         out_shape=[jax.ShapeDtypeStruct(s, F32) for s in shapes],
-        scratch_shapes=[pltpu.VMEM((len(arrays), width, width), F32), pltpu.SemaphoreType.DMA((len(arrays),))],
+        scratch_shapes=[
+            pltpu.VMEM((len(arrays),) + arrays[0].shape, F32),
+            pltpu.SemaphoreType.DMA((len(arrays),)),
+        ],
         input_output_aliases={1 + len(arrays) + i: i for i in range(len(made))},
         cost_estimate=cost(ff * width, 6 * ff * width),
         compiler_params=params(),
@@ -740,7 +745,7 @@
         part = lax.psum_scatter(jnp.concatenate([keep, send], axis=0), axes, scatter_dimension=0, tiled=True)
         return lax.all_gather(part, axes, axis=0, tiled=True)
 
-    blocks = ((0, 0), (0, 1), (1, 0), (1, 1))
+    blocks = ((0, 0, 0), (0, 1, 0), (1, 0, 0), (1, 1, 0))
 
     def placed(kind, pair):
         total = whole_sum(*pair)
@@ -774,6 +779,10 @@
     times = jnp.where((query_ids < count)[None, None, :], 1, times)
     bias = jnp.where(times > 0, jnp.log(jnp.maximum(times, 1).astype(F32)), NEGATIVE)
     return jnp.repeat(bias, BLK, axis=2)
+
+
+def small_outputs(rows):
+    return [rows[24], rows[25], rows[16], rows[17], rows[18], rows[8:12].reshape(-1), rows[3], rows[4], rows[5]]
 
 
 def on_device(
@@ -807,7 +816,7 @@
     rows = tuple(p.shape[0] for p in pieces)
     groups = HEADS // QUAD
     order = Order() if direct else None
-    pairs = ((0, 0), (0, 1), (1, 0), (1, 1))
+    pairs = ((0, 0, 0), (0, 1, 0), (1, 0, 0), (1, 1, 0))
     q, k, v, o, lse = attend(order, pieces, w_query, w_key, w_value, vec, bias)
     layer_out, u1, r1, g_second, g_outer, slope, small_1, hid_t, send_1 = feed(
         order, info, o, x, cotangent.reshape(tok, width), w_out, w_inner, w_outer, vec
@@ -871,21 +880,25 @@
         one.forward()
         (d_outer,) = unpack(order, "rows", info, one.held + one.others, pairs, width, ff)
         three.step()
+        first = swap(three.held[0], 0)
         two.forward()
         (d_inner,) = unpack(order, "cols", info, two.held + two.others, pairs, width, ff)
-        three.step()
-        three.others = [xor_permute(three.held[0], "batch", 1)]
-        made = unpack(order, "four", info, [three.held[0], three.others[0]], pairs[::2], width, ff)
-        three.held[1], *made = lax.optimization_barrier((three.held[1], *made))
-        three.others.append(xor_permute(three.held[1], "batch", 1))
-        made = unpack(order, "four", info, [three.held[1]], pairs[1:2], width, ff, made)
-        d_out, d_query, d_key, d_value = unpack(order, "four", info, [three.others[1]], pairs[3:], width, ff, made)
-        vectors = three.extra
+        vectors = small_outputs(three.extra)
+        three.held[1], vectors, _ = lax.optimization_barrier((three.held[1], vectors, order.last))
+        second = swap(three.held[1], 0)
+        near = three.held + [exchange(a) for a in three.held]
+        made = unpack(order, "four", info, near, ((0, 0, 0), (0, 0, 1), (1, 0, 0), (1, 0, 1)), width, ff)
+        far = [first, exchange(first)]
+        made = unpack(order, "four", info, far, ((0, 1, 0), (1, 1, 0)), width, ff, made)
+        second, made = lax.optimization_barrier((second, made))
+        made = unpack(order, "four", info, [second], ((0, 1, 1),), width, ff, made)
+        last = unpack(order, "four", info, [exchange(second)], ((1, 1, 1),), width, ff, made)
+        d_out, d_query, d_key, d_value = last
     else:
         backs = attend_step()
         keep_3, send_3 = weights_step()
         parts = token_step(tuple(((i, 0),) for i in range(1, shard_count)))
-        vectors = lax.psum(keep_3[2 * width :].astype(F32), ("batch", "seq"))
+        vectors = small_outputs(lax.psum(keep_3[2 * width :].astype(F32), ("batch", "seq")))
         third = (keep_3[: 2 * width], send_3[: 2 * width])
         d_outer, d_inner, d_four, got = summed_plain(
             info, (keep_1, send_1), (keep_2, send_2), third, parts[1:], width, ff
@@ -897,20 +910,20 @@
         layer_out.reshape(1, tok, width),
         token_grad.reshape(1, tok, width),
         d_query,
-        vectors[24],
+        vectors[0],
         d_key,
         d_value,
-        vectors[25],
+        vectors[1],
         d_out,
-        vectors[16],
-        vectors[17],
-        vectors[18],
-        d_inner,
-        vectors[8:12].reshape(-1),
-        d_outer,
+        vectors[2],
         vectors[3],
         vectors[4],
+        d_inner,
         vectors[5],
+        d_outer,
+        vectors[6],
+        vectors[7],
+        vectors[8],
     )
 
 

time: 226 us -> 220 us (0.973)
  waiting for transfers between devices: 70.7 us -> 64 us
  starting transfers between devices: 43.5 us -> 40.2 us
  local copies, waits for them, and re-layouts: 9.3 us -> 11.6 us
    ppermute x26 -> x27, waiting for transfers between devices: 65.1 us -> 58.6 us  [swap(): return lax.ppermute(value, ('batch', 'seq'), pairs)]
    ppermute x26 -> x27, starting transfers between devices: 35.3 us -> 30.7 us  [swap(): return lax.ppermute(value, ('batch', 'seq'), pairs)]
    ppermute x13 -> x15, starting transfers between devices: 8.2 us -> 9.57 us  [xor_permute(): return lax.ppermute(value, axis, [(i, i ^ mask) for i in range(size)])]
    ppermute x13 -> x15, waiting for transfers between devices: 5.59 us -> 5.35 us  [xor_permute(): return lax.ppermute(value, axis, [(i, i ^ mask) for i in range(size)])]
    unnamed x44 -> x46, local copies, waits for them, and re-layouts: 5.63 us -> 5.64 us
  transfers between devices with their start and end apart: 39 -> 42, of which waited for: 17 -> 18; matrix products, arithmetic and copies ran while one was open for 4% -> 5% of each run, Pallas kernels for 34% -> 36%
where the time goes in v2:
time: 220 us; the launch traced here: 219 us
  Pallas kernels  101 us (46%)
  waiting for transfers between devices  64 us (29%)
  starting transfers between devices  40.2 us (18%)
  local copies, waits for them, and re-layouts  11.6 us (5%)
    pallas_call x38, Pallas kernels, ordered(): pl.pallas_call(kernel, in_specs=list(in_specs) + [pl.BlockSpec(memory_spa...  101 us
    ppermute x27, waiting for transfers between devices, swap(): return lax.ppermute(value, ('batch', 'seq'), pairs)  58.6 us
    ppermute x27, starting transfers between devices, swap(): return lax.ppermute(value, ('batch', 'seq'), pairs)  30.7 us
    ppermute x15, starting transfers between devices, xor_permute(): return lax.ppermute(value, axis, [(i, i ^ mask) for i in range(size)])  9.57 us
    unnamed x46, local copies, waits for them, and re-layouts  5.64 us
    ppermute x15, waiting for transfers between devices, xor_permute(): return lax.ppermute(value, axis, [(i, i ^ mask) for i in range(size)])  5.35 us
  transfers between devices with their start and end apart: 42, of which 18 were waited for; matrix products, arithmetic and copies ran while one was open for 5% of the time, Pallas kernels for 36%

profile of v2, /device:TPU:0, one launch (start us, length us, event | category | flops | bytes accessed | tf_op | source)
XLA Modules:
  0.0 219.3 jit_solution(14658591436288743640)
XLA Ops:
  0.7 3.0 %collective-permute-start.1 = (bf16[256,768]{1,0:T(8,128)(2,1)}, bf16[256,768]{1,0:T(8,128)(2,1)S(1)}, u32[]{:S(2)}, u32[]{:S(2)}) collective-permute-start(bf16[256,768]{1,0:T(8,128)(2,1)} %bitcast.20), channel_id=1, source_target_pairs={{0,2},{1,3},{2,0},{3,1},{4,6},{5,7},{6,4},{7,5},{8,10},{9,11},{10,... | collective-permute-start | bytes 1179656 | tf_op jit(solution)/shard_map/ppermute | solution.py:582
  20.6 12.4 %attend.1 = (bf16[256,768]{1,0:T(8,128)(2,1)}, bf16[3,1024,256]{2,1,0:T(8,128)(2,1)}, bf16[3,1024,256]{2,1,0:T(8,128)(2,1)}, f32[256,768]{1,0:T(8,128)S(1)}, f32...) custom-call(bf16[256,768]{1,0:T(8,128)(2,1)S(1)} %bitcast.22, bf16[256,768]{1,0:T(8,128)(2,1)S(1)} %collective-permute-done.refs_1_.refs_9_, ...), custom_call_target="tpu_custom_call" | custom-call | flops 563714457600 | bytes 629145600 | tf_op jit(solution)/shard_map/attend/pallas_call | solution.py:58
  33.1 8.1 %feed.1 = (bf16[256,768]{1,0:T(8,128)(2,1)}, f32[256,768]{1,0:T(8,128)S(1)}, f32[256,128]{1,0:T(8,128)S(1)}, f32[256,768]{1,0:T(8,128)S(1)}, bf16[256,768]{1,0:T...) custom-call(s32[7]{0:T(128)S(1)} %stack.39.refs_0_, ...), custom_call_target="tpu_custom_call" | custom-call | flops 332188876800 | bytes 1887436800 | tf_op jit(solution)/shard_map/feed/pallas_call | solution.py:58
  41.2 6.6 %inner_back.1 = (bf16[1536,768]{1,0:T(8,128)(2,1)}, bf16[256,3072]{1,0:T(8,128)(2,1)S(1)}, bf16[2,768,256]{2,1,0:T(8,128)(2,1)S(1)}, f32[256,768]{1,0:T(8,128)S(...) custom-call(s32[7]{0:T(128)S(1)} %stack.39.refs_0_, ...), custom_call_target="tpu_custom_call" | custom-call | flops 362387865600 | bytes 1887436800 | tf_op jit(solution)/shard_map/inner_back/pallas_call | solution.py:58
  51.6 4.3 %branch_back.1 = (bf16[1536,768]{1,0:T(8,128)(2,1)}, f32[256,768]{1,0:T(8,128)}, bf16[256,768]{1,0:T(8,128)(2,1)}, f32[16,256]{1,0:T(8,128)S(1)}, f32[8,768]{1,0...) custom-call(s32[7]{0:T(128)S(1)} %stack.39.refs_0_, f32[256,768]{1,0:T(8,128)S(1)} %copy-done.18, ...), custom_call_target="tpu_custom_call" | custom-call | flops 120795955200 | bytes 943718400 | tf_op jit(solution)/shard_map/branch_back/pallas_call | solution.py:58
  55.9 2.9 %combine.14 = (bf16[768,768]{1,0:T(8,128)(2,1)}, f32[8,128]{1,0:T(8,128)S(1)}) custom-call(bf16[1536,768]{1,0:T(8,128)(2,1)} %get-tuple-element.171.refs_0_, bf16[1536,768]{1,0:T(8,128)(2,1)} %collective-permute-done.5.refs_1_, f32[8,128]{1,0:T(8,128)S(1)} %get-tuple-element.173.refs_2_), custom_call_target="tpu_custom_call" | custom-call | flops 4300000256 | bytes 104857600 | tf_op jit(solution)/shard_map/combine/pallas_call | solution.py:58
  59.7 12.8 %attend_back.1 = (bf16[3,256,256]{2,1,0:T(8,128)(2,1)S(1)}, bf16[3,1024,256]{2,1,0:T(8,128)(2,1)S(1)}, bf16[3,1024,256]{2,1,0:T(8,128)(2,1)S(1)}, f32[8,128]{1,0:T(8,128)S(1)}) custom-call(bf16[256,768]{1,0:T(8,128)(2,1)} %get-tuple-element.165.refs_0_, bf16[3,1024,256]{2,1,0:T(8,128)(2,1)} %get-tuple-element.166.refs_1_, ...), custom_call_target="tpu_custom_call" | custom-call | flops 5000000000 | bytes 104857600 | tf_op jit(solution)/shard_map/attend_back/pallas_call | solution.py:58
  76.6 6.6 %weights.1 = (bf16[1568,768]{1,0:T(8,128)(2,1)}, bf16[1568,768]{1,0:T(8,128)(2,1)}, f32[8,128]{1,0:T(8,128)S(1)}) custom-call(s32[7]{0:T(128)S(1)} %stack.39.refs_0_, bf16[768,768]{1,0:T(8,128)(2,1)S(1)} %copy-done.15, f32[8,768]{1,0:T(8,128)S(1)} %get-tuple-element.183.refs_2_, f32[8,768]{1,0:T(8,128)S(1)} %get-tuple-element.184.refs_3_, ...), custom_call_target="tpu_custom_call" | custom-call | flops 271790899200 | bytes 943718400 | tf_op jit(solution)/shard_map/weights/pallas_call | solution.py:58
  89.9 3.5 %token_parts.1 = (f32[256,768]{1,0:T(8,128)S(1)}, bf16[512,768]{1,0:T(8,128)(2,1)S(1)}, bf16[256,768]{1,0:T(8,128)(2,1)S(1)}, f32[8,128]{1,0:T(8,128)S(1)}) custom-call(s32[7]{0:T(128)S(1)} %stack.39.refs_0_, bf16[768,768]{1,0:T(8,128)(2,1)S(1)} %copy-done.5, bf16[768,768]{1,0:T(8,128)(2,1)S(1)} %copy-done.6, bf16[768,768]{1,0:T(8,128)(2,1)S(1)} %copy-done.7, ...), custom_call_target="tpu_custom_call" | custom-call | flops 271790899200 | bytes 943718400 | tf_op jit(solution)/shard_map/token_parts/pallas_call | solution.py:58
  100.5 2.7 %collective-permute-start.12 = (bf16[96,768]{1,0:T(8,128)(2,1)S(1)}, bf16[96,768]{1,0:T(8,128)(2,1)S(1)}, u32[]{:S(2)}, u32[]{:S(2)}) collective-permute-start(bf16[96,768]{1,0:T(8,128)(2,1)S(1)} %get-tuple-element.197), channel_id=1, source_target_pairs={{0,16},{1,17},{2,18},{3,19},{4,12},{5,13},{6,14},{7,15},{8,24},{9,... | collective-permute-start | bytes 442376 | tf_op jit(solution)/shard_map/ppermute | solution.py:705
  111.7 2.9 %collective-permute-start.17 = (bf16[96,768]{1,0:T(8,128)(2,1)S(1)}, bf16[96,768]{1,0:T(8,128)(2,1)S(1)}, u32[]{:S(2)}, u32[]{:S(2)}) collective-permute-start(bf16[96,768]{1,0:T(8,128)(2,1)S(1)} %get-tuple-element.207.refs_0_), channel_id=1, source_target_pairs={{0,16},{1,17},{2,18},{3,19},{4,12},{5,13},{6,14},{7,15},{8,24},{9,... | collective-permute-start | bytes 442376 | tf_op jit(solution)/shard_map/ppermute | solution.py:705
  115.6 7.7 %collective-permute-done.18.refs_5_ = bf16[96,768]{1,0:T(8,128)(2,1)S(1)} collective-permute-done((bf16[96,768]{1,0:T(8,128)(2,1)S(1)}, bf16[96,768]{1,0:T(8,128)(2,1)S(1)}, u32[]{:S(2)}, u32[]{:S(2)}) %collective-permute-start.18) | collective-permute-done | bytes 147488 | tf_op jit(solution)/shard_map/ppermute | solution.py:705
  124.7 3.7 %collective-permute-start.20 = (bf16[192,768]{1,0:T(8,128)(2,1)S(1)}, bf16[192,768]{1,0:T(8,128)(2,1)S(1)}, u32[]{:S(2)}, u32[]{:S(2)}) collective-permute-start(bf16[192,768]{1,0:T(8,128)(2,1)S(1)} %get-tuple-element.215.refs_0_), channel_id=1, source_target_pairs={{0,8},{1,9},{2,10},{3,11},{4,20},{5,21},{6,22},{7,23},{8,0},{9,1},... | collective-permute-start | bytes 884744 | tf_op jit(solution)/shard_map/ppermute | solution.py:705
  131.4 4.2 %collective-permute-done.21.refs_1_ = bf16[96,768]{1,0:T(8,128)(2,1)S(1)} collective-permute-done((bf16[96,768]{1,0:T(8,128)(2,1)S(1)}, bf16[96,768]{1,0:T(8,128)(2,1)S(1)}, u32[]{:S(2)}, u32[]{:S(2)}) %collective-permute-start.21) | collective-permute-done | bytes 147488 | tf_op jit(solution)/shard_map/ppermute | solution.py:705
  136.8 3.4 %collective-permute-done.19.refs_3_.refs_5_ = bf16[416,768]{1,0:T(8,128)(2,1)S(1)} collective-permute-done((bf16[416,768]{1,0:T(8,128)(2,1)S(1)}, bf16[416,768]{1,0:T(8,128)(2,1)S(1)}, u32[]{:S(2)}, u32[]{:S(2)}) %collective-permute-start.19) | collective-permute-done | bytes 639008 | tf_op jit(solution)/shard_map/ppermute | solution.py:705
  143.4 4.5 %collective-permute-done.23.refs_1_ = bf16[384,768]{1,0:T(8,128)(2,1)S(1)} collective-permute-done((bf16[384,768]{1,0:T(8,128)(2,1)S(1)}, bf16[384,768]{1,0:T(8,128)(2,1)S(1)}, u32[]{:S(2)}, u32[]{:S(2)}) %collective-permute-start.23) | collective-permute-done | bytes 589856 | tf_op jit(solution)/shard_map/ppermute | solution.py:705
  154.2 12.3 %collective-permute-done.26.refs_1_ = bf16[384,768]{1,0:T(8,128)(2,1)S(1)} collective-permute-done((bf16[384,768]{1,0:T(8,128)(2,1)S(1)}, bf16[384,768]{1,0:T(8,128)(2,1)S(1)}, u32[]{:S(2)}, u32[]{:S(2)}) %collective-permute-start.26) | collective-permute-done | bytes 589856 | tf_op jit(solution)/shard_map/ppermute | solution.py:705
  168.4 3.4 %collective-permute-start.27 = (bf16[96,768]{1,0:T(8,128)(2,1)S(1)}, bf16[96,768]{1,0:T(8,128)(2,1)S(1)}, u32[]{:S(2)}, u32[]{:S(2)}) collective-permute-start(bf16[96,768]{1,0:T(8,128)(2,1)S(1)} %get-tuple-element.230.refs_0_), channel_id=1, source_target_pairs={{0,16},{1,17},{2,18},{3,19},{4,12},{5,13},{6,14},{7,15},{8,24},{9,... | collective-permute-start | bytes 442376 | tf_op jit(solution)/shard_map/ppermute | solution.py:705
  171.8 4.0 %collective-permute-done.27.refs_1_ = bf16[96,768]{1,0:T(8,128)(2,1)S(1)} collective-permute-done((bf16[96,768]{1,0:T(8,128)(2,1)S(1)}, bf16[96,768]{1,0:T(8,128)(2,1)S(1)}, u32[]{:S(2)}, u32[]{:S(2)}) %collective-permute-start.27) | collective-permute-done | bytes 147488 | tf_op jit(solution)/shard_map/ppermute | solution.py:705
  177.7 5.2 %collective-permute-done.33.refs_2_ = bf16[768,768]{1,0:T(8,128)(2,1)S(1)} collective-permute-done((bf16[768,768]{1,0:T(8,128)(2,1)S(1)}, bf16[768,768]{1,0:T(8,128)(2,1)S(1)}, u32[]{:S(2)}, u32[]{:S(2)}) %collective-permute-start.33) | collective-permute-done | bytes 1179680 | tf_op jit(solution)/shard_map/ppermute | solution.py:705
  182.9 4.4 %unpack_rows.1 = (f32[3072,768]{1,0:T(8,128)}, f32[8,128]{1,0:T(8,128)S(1)}) custom-call(s32[7]{0:T(128)S(1)} %stack.39.refs_0_, bf16[768,768]{1,0:T(8,128)(2,1)S(1)} %get-tuple-element.233.refs_1_, bf16[768,768]{1,0:T(8,128)(2,1)S(1)} %collective-permute-done.29.refs_2_, bf16[768,768]{1,0:T(8,128)(2,1)S(1)} %collective-permute-done.30.refs_3_, ...), custom_call_target="tpu_custom_call" | custom-call | flops 235929600 | bytes 1415577600 | tf_op jit(solution)/shard_map/unpack_rows/pallas_call | solution.py:58
  192.3 5.1 %unpack_cols.1 = (f32[768,3072]{1,0:T(8,128)}, f32[8,128]{1,0:T(8,128)S(1)}) custom-call(s32[7]{0:T(128)S(1)} %stack.39.refs_0_, bf16[768,768]{1,0:T(8,128)(2,1)S(1)} %get-tuple-element.238.refs_1_, bf16[768,768]{1,0:T(8,128)(2,1)S(1)} %collective-permute-done.33.refs_2_, bf16[768,768]{1,0:T(8,128)(2,1)S(1)} %collective-permute-done.34.refs_3_, ...), custom_call_target="tpu_custom_call" | custom-call | flops 235929600 | bytes 1415577600 | tf_op jit(solution)/shard_map/unpack_cols/pallas_call | solution.py:58
  197.4 6.8 %collective-permute-done.32.refs_2_ = bf16[384,768]{1,0:T(8,128)(2,1)} collective-permute-done((bf16[384,768]{1,0:T(8,128)(2,1)}, bf16[384,768]{1,0:T(8,128)(2,1)}, u32[]{:S(2)}, u32[]{:S(2)}) %collective-permute-start.32) | collective-permute-done | bytes 589856 | tf_op jit(solution)/shard_map/ppermute | solution.py:705
  206.5 3.5 %unpack_four.4 = (f32[768,768]{1,0:T(8,128)}, f32[768,768]{1,0:T(8,128)}, f32[768,768]{1,0:T(8,128)}, f32[768,768]{1,0:T(8,128)}, f32[8,128]{1,0:T(8,128)S(1)}) custom-call(s32[7]{0:T(128)S(1)} %stack.39.refs_0_, bf16[384,768]{1,0:T(8,128)(2,1)} %get-tuple-element.236.refs_1_, bf16[384,768]{1,0:T(8,128)(2,1)} %collective-permute-done.32.refs_2_, ...), custom_call_target="tpu_custom_call" | custom-call | flops 235929600 | bytes 1415577600 | tf_op jit(solution)/shard_map/unpack_four/pallas_call | solution.py:58
  (167 shorter events, 83.2 us)
Async XLA Ops:
  0.7 12.6 %collective-permute-start.1 = (bf16[256,768]{1,0:T(8,128)(2,1)}, bf16[256,768]{1,0:T(8,128)(2,1)S(1)}, u32[]{:S(2)}, u32[]{:S(2)}) collective-permute-start(bf16[256,768]{1,0:T(8,128)(2,1)} %bitcast.20), channel_id=1, source_target_pairs={{0,2},{1,3},{2,0},{3,1},{4,6},{5,7},{6,4},{7,5},{8,10},{9,11},{10,... | collective-permute-start | bytes 1179656 | tf_op jit(solution)/shard_map/ppermute | solution.py:582
  3.7 11.1 %collective-permute-start = (bf16[256,768]{1,0:T(8,128)(2,1)}, bf16[256,768]{1,0:T(8,128)(2,1)S(1)}, u32[]{:S(2)}, u32[]{:S(2)}) collective-permute-start(bf16[256,768]{1,0:T(8,128)(2,1)} %bitcast.21), channel_id=1, source_target_pairs={{0,1},{1,0},{2,3},{3,2},{4,5},{5,4},{6,7},{7,6},{8,9},{9,8},{10,11... | collective-permute-start | bytes 1179656 | tf_op jit(solution)/shard_map/ppermute | solution.py:582
  50.4 22.2 %collective-permute-start.6 = (bf16[768,768]{1,0:T(8,128)(2,1)S(1)}, bf16[768,768]{1,0:T(8,128)(2,1)S(1)}, u32[]{:S(2)}, u32[]{:S(2)}) collective-permute-start(bf16[768,768]{1,0:T(8,128)(2,1)S(1)} %get-tuple-element.178), channel_id=1, source_target_pairs={{0,1},{1,0},{2,3},{3,2},{4,6},{5,7},{6,4},{7,5},{8,9},{9,8},{10,11... | collective-permute-start | bytes 3538952 | tf_op jit(solution)/shard_map/ppermute | solution.py:705
  58.8 24.3 %collective-permute-start.8 = (bf16[768,768]{1,0:T(8,128)(2,1)}, bf16[768,768]{1,0:T(8,128)(2,1)}, u32[]{:S(2)}, u32[]{:S(2)}) collective-permute-start(bf16[768,768]{1,0:T(8,128)(2,1)} %get-tuple-element.181), channel_id=1, source_target_pairs={{0,1},{1,0},{2,3},{3,2},{4,6},{5,7},{6,4},{7,5},{8,9},{9,8},{10,11... | collective-permute-start | bytes 3538952 | tf_op jit(solution)/shard_map/ppermute | solution.py:705
  75.0 11.1 %collective-permute-start.7 = (bf16[384,768]{1,0:T(8,128)(2,1)}, bf16[384,768]{1,0:T(8,128)(2,1)}, u32[]{:S(2)}, u32[]{:S(2)}) collective-permute-start(bf16[384,768]{1,0:T(8,128)(2,1)} %get-tuple-element.180), channel_id=1, source_target_pairs={{0,2},{1,3},{2,0},{3,1},{4,5},{5,4},{6,7},{7,6},{8,10},{9,11},{10,... | collective-permute-start | bytes 1769480 | tf_op jit(solution)/shard_map/ppermute | solution.py:705
  86.1 17.1 %collective-permute-start.14 = (bf16[1568,768]{1,0:T(8,128)(2,1)}, bf16[1568,768]{1,0:T(8,128)(2,1)}, u32[]{:S(2)}, u32[]{:S(2)}) collective-permute-start(bf16[1568,768]{1,0:T(8,128)(2,1)} %get-tuple-element.200), channel_id=1, source_target_pairs={{0,4},{4,0},{8,12},{12,8},{16,20},{20,16},{24,28},{28,24},{1,5},{5... | collective-permute-start | bytes 7225352 | tf_op jit(solution)/shard_map/ppermute | solution.py:582
  97.2 12.0 %collective-permute-start.13 = (bf16[192,768]{1,0:T(8,128)(2,1)S(1)}, bf16[192,768]{1,0:T(8,128)(2,1)S(1)}, u32[]{:S(2)}, u32[]{:S(2)}) collective-permute-start(bf16[192,768]{1,0:T(8,128)(2,1)S(1)} %get-tuple-element.198), channel_id=1, source_target_pairs={{0,8},{1,9},{2,10},{3,11},{4,20},{5,21},{6,22},{7,23},{8,0},{9,1},... | collective-permute-start | bytes 884744 | tf_op jit(solution)/shard_map/ppermute | solution.py:705
  98.8 15.8 %collective-permute-start.9 = (bf16[512,768]{1,0:T(8,128)(2,1)S(1)}, bf16[512,768]{1,0:T(8,128)(2,1)S(1)}, u32[]{:S(2)}, u32[]{:S(2)}) collective-permute-start(bf16[512,768]{1,0:T(8,128)(2,1)S(1)} %get-tuple-element.191), channel_id=1, source_target_pairs={{0,1},{1,0},{2,3},{3,2},{4,6},{5,7},{6,4},{7,5},{8,9},{9,8},{10,11... | collective-permute-start | bytes 2359304 | tf_op jit(solution)/shard_map/ppermute | solution.py:705
  105.1 23.2 %collective-permute-start.16 = (bf16[800,768]{1,0:T(8,128)(2,1)S(1)}, bf16[800,768]{1,0:T(8,128)(2,1)S(1)}, u32[]{:S(2)}, u32[]{:S(2)}) collective-permute-start(bf16[800,768]{1,0:T(8,128)(2,1)S(1)} %get-tuple-element.206.refs_3_), channel_id=1, source_target_pairs={{0,1},{1,0},{2,3},{3,2},{4,6},{5,7},{6,4},{7,5},{8,9},{9,8},{10,11... | collective-permute-start | bytes 3686408 | tf_op jit(solution)/shard_map/ppermute | solution.py:705
  111.7 13.0 %collective-permute-start.17 = (bf16[96,768]{1,0:T(8,128)(2,1)S(1)}, bf16[96,768]{1,0:T(8,128)(2,1)S(1)}, u32[]{:S(2)}, u32[]{:S(2)}) collective-permute-start(bf16[96,768]{1,0:T(8,128)(2,1)S(1)} %get-tuple-element.207.refs_0_), channel_id=1, source_target_pairs={{0,16},{1,17},{2,18},{3,19},{4,12},{5,13},{6,14},{7,15},{8,24},{9,... | collective-permute-start | bytes 442376 | tf_op jit(solution)/shard_map/ppermute | solution.py:705
  114.8 15.6 %collective-permute-start.15 = (bf16[256,768]{1,0:T(8,128)(2,1)S(1)}, bf16[256,768]{1,0:T(8,128)(2,1)S(1)}, u32[]{:S(2)}, u32[]{:S(2)}) collective-permute-start(bf16[256,768]{1,0:T(8,128)(2,1)S(1)} %get-tuple-element.205), channel_id=1, source_target_pairs={{0,2},{1,3},{2,0},{3,1},{4,5},{5,4},{6,7},{7,6},{8,10},{9,11},{10,... | collective-permute-start | bytes 1179656 | tf_op jit(solution)/shard_map/ppermute | solution.py:705
  124.7 11.5 %collective-permute-start.20 = (bf16[192,768]{1,0:T(8,128)(2,1)S(1)}, bf16[192,768]{1,0:T(8,128)(2,1)S(1)}, u32[]{:S(2)}, u32[]{:S(2)}) collective-permute-start(bf16[192,768]{1,0:T(8,128)(2,1)S(1)} %get-tuple-element.215.refs_0_), channel_id=1, source_target_pairs={{0,8},{1,9},{2,10},{3,11},{4,20},{5,21},{6,22},{7,23},{8,0},{9,1},... | collective-permute-start | bytes 884744 | tf_op jit(solution)/shard_map/ppermute | solution.py:705
  136.2 11.7 %collective-permute-start.23 = (bf16[384,768]{1,0:T(8,128)(2,1)S(1)}, bf16[384,768]{1,0:T(8,128)(2,1)S(1)}, u32[]{:S(2)}, u32[]{:S(2)}) collective-permute-start(bf16[384,768]{1,0:T(8,128)(2,1)S(1)} %get-tuple-element.221.refs_0_), channel_id=1, source_target_pairs={{0,2},{1,3},{2,0},{3,1},{4,5},{5,4},{6,7},{7,6},{8,10},{9,11},{10,... | collective-permute-start | bytes 1769480 | tf_op jit(solution)/shard_map/ppermute | solution.py:705
  148.1 18.7 %collective-permute-start.29 = (bf16[768,768]{1,0:T(8,128)(2,1)S(1)}, bf16[768,768]{1,0:T(8,128)(2,1)S(1)}, u32[]{:S(2)}, u32[]{:S(2)}) collective-permute-start(bf16[768,768]{1,0:T(8,128)(2,1)S(1)} %get-tuple-element.233.refs_1_), channel_id=1, source_target_pairs={{0,1},{1,0},{2,3},{3,2},{4,6},{5,7},{6,4},{7,5},{8,9},{9,8},{10,11... | collective-permute-start | bytes 3538952 | tf_op jit(solution)/shard_map/ppermute | solution.py:705
  150.3 16.3 %collective-permute-start.26 = (bf16[384,768]{1,0:T(8,128)(2,1)S(1)}, bf16[384,768]{1,0:T(8,128)(2,1)S(1)}, u32[]{:S(2)}, u32[]{:S(2)}) collective-permute-start(bf16[384,768]{1,0:T(8,128)(2,1)S(1)} %get-tuple-element.227.refs_0_), channel_id=1, source_target_pairs={{0,2},{1,3},{2,0},{3,1},{4,5},{5,4},{6,7},{7,6},{8,10},{9,11},{10,... | collective-permute-start | bytes 1769480 | tf_op jit(solution)/shard_map/ppermute | solution.py:705
  152.6 14.7 %collective-permute-start.25 = (bf16[128,768]{1,0:T(8,128)(2,1)S(1)}, bf16[128,768]{1,0:T(8,128)(2,1)S(1)}, u32[]{:S(2)}, u32[]{:S(2)}) collective-permute-start(bf16[128,768]{1,0:T(8,128)(2,1)S(1)} %get-tuple-element.226.refs_6_), channel_id=1, source_target_pairs={{0,16},{1,17},{2,18},{3,19},{4,12},{5,13},{6,14},{7,15},{8,24},{9,... | collective-permute-start | bytes 589832 | tf_op jit(solution)/shard_map/ppermute | solution.py:705
  166.6 16.3 %collective-permute-start.33 = (bf16[768,768]{1,0:T(8,128)(2,1)S(1)}, bf16[768,768]{1,0:T(8,128)(2,1)S(1)}, u32[]{:S(2)}, u32[]{:S(2)}) collective-permute-start(bf16[768,768]{1,0:T(8,128)(2,1)S(1)} %get-tuple-element.238.refs_1_), channel_id=1, source_target_pairs={{0,1},{1,0},{2,3},{3,2},{4,6},{5,7},{6,4},{7,5},{8,9},{9,8},{10,11... | collective-permute-start | bytes 3538952 | tf_op jit(solution)/shard_map/ppermute | solution.py:705
  166.8 16.1 %collective-permute-start.30 = (bf16[768,768]{1,0:T(8,128)(2,1)S(1)}, bf16[768,768]{1,0:T(8,128)(2,1)S(1)}, u32[]{:S(2)}, u32[]{:S(2)}) collective-permute-start(bf16[768,768]{1,0:T(8,128)(2,1)S(1)} %get-tuple-element.233.refs_1_), channel_id=1, source_target_pairs={{0,4},{4,0},{8,12},{12,8},{16,20},{20,16},{24,28},{28,24},{1,5},{5... | collective-permute-start | bytes 3538952 | tf_op jit(solution)/shard_map/ppermute | solution.py:582
  166.8 16.1 %collective-permute-start.31 = (bf16[768,768]{1,0:T(8,128)(2,1)S(1)}, bf16[768,768]{1,0:T(8,128)(2,1)S(1)}, u32[]{:S(2)}, u32[]{:S(2)}) collective-permute-start(bf16[768,768]{1,0:T(8,128)(2,1)S(1)} %collective-permute-done.29.refs_2_), channel_id=1, source_target_pairs={{0,4},{4,0},{8,12},{12,8},{16,20},{20,16},{24,28},{28,24},{1,5},{5... | collective-permute-start | bytes 3538952 | tf_op jit(solution)/shard_map/ppermute | solution.py:582
  175.8 11.6 %collective-permute-start.28 = (bf16[192,768]{1,0:T(8,128)(2,1)S(1)}, bf16[192,768]{1,0:T(8,128)(2,1)S(1)}, u32[]{:S(2)}, u32[]{:S(2)}) collective-permute-start(bf16[192,768]{1,0:T(8,128)(2,1)S(1)} %get-tuple-element.232.refs_0_), channel_id=1, source_target_pairs={{0,8},{1,9},{2,10},{3,11},{4,20},{5,21},{6,22},{7,23},{8,0},{9,1},... | collective-permute-start | bytes 884744 | tf_op jit(solution)/shard_map/ppermute | solution.py:705
  177.7 14.5 %collective-permute-start.34 = (bf16[768,768]{1,0:T(8,128)(2,1)S(1)}, bf16[768,768]{1,0:T(8,128)(2,1)S(1)}, u32[]{:S(2)}, u32[]{:S(2)}) collective-permute-start(bf16[768,768]{1,0:T(8,128)(2,1)S(1)} %get-tuple-element.238.refs_1_), channel_id=1, source_target_pairs={{0,4},{4,0},{8,12},{12,8},{16,20},{20,16},{24,28},{28,24},{1,5},{5... | collective-permute-start | bytes 3538952 | tf_op jit(solution)/shard_map/ppermute | solution.py:582
  188.2 16.1 %collective-permute-start.32 = (bf16[384,768]{1,0:T(8,128)(2,1)}, bf16[384,768]{1,0:T(8,128)(2,1)}, u32[]{:S(2)}, u32[]{:S(2)}) collective-permute-start(bf16[384,768]{1,0:T(8,128)(2,1)} %get-tuple-element.236.refs_1_), channel_id=1, source_target_pairs={{0,2},{1,3},{2,0},{3,1},{4,5},{5,4},{6,7},{7,6},{8,10},{9,11},{10,... | collective-permute-start | bytes 1769480 | tf_op jit(solution)/shard_map/ppermute | solution.py:705
  188.2 16.1 %collective-permute-start.37 = (bf16[384,768]{1,0:T(8,128)(2,1)}, bf16[384,768]{1,0:T(8,128)(2,1)}, u32[]{:S(2)}, u32[]{:S(2)}) collective-permute-start(bf16[384,768]{1,0:T(8,128)(2,1)} %get-tuple-element.236.refs_1_), channel_id=1, source_target_pairs={{0,1},{1,0},{2,3},{3,2},{4,6},{5,7},{6,4},{7,5},{8,9},{9,8},{10,11... | collective-permute-start | bytes 1769480 | tf_op jit(solution)/shard_map/ppermute | solution.py:705
  191.8 13.0 %collective-permute-start.39 = (bf16[384,768]{1,0:T(8,128)(2,1)}, bf16[384,768]{1,0:T(8,128)(2,1)S(1)}, u32[]{:S(2)}, u32[]{:S(2)}) collective-permute-start(bf16[384,768]{1,0:T(8,128)(2,1)} %get-tuple-element.236.refs_1_), channel_id=1, source_target_pairs={{0,4},{4,0},{8,12},{12,8},{16,20},{20,16},{24,28},{28,24},{1,5},{5... | collective-permute-start | bytes 1769480 | tf_op jit(solution)/shard_map/ppermute | solution.py:582
  (37 other events, 304.1 us)

commit v3 on v2

--- a/solution.py
+++ b/solution.py
@@ -607,14 +607,20 @@
     width = ways[0][0][0].shape[1]
     terms = [t for way in ways for t in way]
     made = jax.ShapeDtypeStruct((count + (32 if extras else 0), width), BF)
+    steps = 1 if extras or count < 384 else 2
+    part = count // steps
+
+    def at(index):
+        return pl.BlockSpec((part, width), lambda i: (index * steps + i, 0))
+
     return ordered(
         functools.partial(combine_body, len(ways), len(ways[0]), len(extras)),
         order,
-        [rows_at(count, i) for _, i in terms] + [rows_at(32, i) for _, i in extras],
+        [at(i) for _, i in terms] + [rows_at(32, i) for _, i in extras],
         (*(in_hbm(a) for a, _ in terms), *(in_hbm(a) for a, _ in extras)),
         "combine",
-        grid=(1,),
-        out_specs=[pl.BlockSpec(made.shape, lambda *_: (0, 0))] * len(ways),
+        grid=(steps,),
+        out_specs=[pl.BlockSpec((made.shape[0] // steps, width), lambda i: (i, 0))] * len(ways),
         out_shape=[made] * len(ways),
         cost_estimate=cost(EVENT_FLOPS, 1 << 20),
         compiler_params=params(),

time: 220 us -> 220 us (level)
  transfers between devices with their start and end apart: 42 -> 42, of which waited for: 18 -> 17; matrix products, arithmetic and copies ran while one was open for 5% -> 5% of each run, Pallas kernels for 36% -> 36%
where the time goes in v3:
time: 220 us; the launch traced here: 219 us
  Pallas kernels  101 us (46%)
  waiting for transfers between devices  62.7 us (28%)
  starting transfers between devices  41.8 us (19%)
  local copies, waits for them, and re-layouts  11.6 us (5%)
    pallas_call x38, Pallas kernels, ordered(): pl.pallas_call(kernel, in_specs=list(in_specs) + [pl.BlockSpec(memory_spa...  101 us
    ppermute x27, waiting for transfers between devices, swap(): return lax.ppermute(value, ('batch', 'seq'), pairs)  57.4 us
    ppermute x27, starting transfers between devices, swap(): return lax.ppermute(value, ('batch', 'seq'), pairs)  32.6 us
    ppermute x15, starting transfers between devices, xor_permute(): return lax.ppermute(value, axis, [(i, i ^ mask) for i in range(size)])  9.15 us
    unnamed x46, local copies, waits for them, and re-layouts  5.64 us
    ppermute x15, waiting for transfers between devices, xor_permute(): return lax.ppermute(value, axis, [(i, i ^ mask) for i in range(size)])  5.3 us
  transfers between devices with their start and end apart: 42, of which 17 were waited for; matrix products, arithmetic and copies ran while one was open for 5% of the time, Pallas kernels for 36%

profile of v3, /device:TPU:0, one launch (start us, length us, event | category | flops | bytes accessed | tf_op | source)
XLA Modules:
  0.0 218.9 jit_solution(10321588830669884516)
XLA Ops:
  0.7 3.0 %collective-permute-start.1 = (bf16[256,768]{1,0:T(8,128)(2,1)}, bf16[256,768]{1,0:T(8,128)(2,1)S(1)}, u32[]{:S(2)}, u32[]{:S(2)}) collective-permute-start(bf16[256,768]{1,0:T(8,128)(2,1)} %bitcast.20), channel_id=1, source_target_pairs={{0,2},{1,3},{2,0},{3,1},{4,6},{5,7},{6,4},{7,5},{8,10},{9,11},{10,... | collective-permute-start | bytes 1179656 | tf_op jit(solution)/shard_map/ppermute | solution.py:582
  20.6 12.4 %attend.1 = (bf16[256,768]{1,0:T(8,128)(2,1)}, bf16[3,1024,256]{2,1,0:T(8,128)(2,1)}, bf16[3,1024,256]{2,1,0:T(8,128)(2,1)}, f32[256,768]{1,0:T(8,128)S(1)}, f32...) custom-call(bf16[256,768]{1,0:T(8,128)(2,1)S(1)} %bitcast.22, bf16[256,768]{1,0:T(8,128)(2,1)S(1)} %collective-permute-done.refs_1_.refs_9_, ...), custom_call_target="tpu_custom_call" | custom-call | flops 563714457600 | bytes 629145600 | tf_op jit(solution)/shard_map/attend/pallas_call | solution.py:58
  33.1 8.1 %feed.1 = (bf16[256,768]{1,0:T(8,128)(2,1)}, f32[256,768]{1,0:T(8,128)S(1)}, f32[256,128]{1,0:T(8,128)S(1)}, f32[256,768]{1,0:T(8,128)S(1)}, bf16[256,768]{1,0:T...) custom-call(s32[7]{0:T(128)S(1)} %stack.39.refs_0_, ...), custom_call_target="tpu_custom_call" | custom-call | flops 332188876800 | bytes 1887436800 | tf_op jit(solution)/shard_map/feed/pallas_call | solution.py:58
  41.2 6.6 %inner_back.1 = (bf16[1536,768]{1,0:T(8,128)(2,1)}, bf16[256,3072]{1,0:T(8,128)(2,1)S(1)}, bf16[2,768,256]{2,1,0:T(8,128)(2,1)S(1)}, f32[256,768]{1,0:T(8,128)S(...) custom-call(s32[7]{0:T(128)S(1)} %stack.39.refs_0_, ...), custom_call_target="tpu_custom_call" | custom-call | flops 362387865600 | bytes 1887436800 | tf_op jit(solution)/shard_map/inner_back/pallas_call | solution.py:58
  51.7 4.3 %branch_back.1 = (bf16[1536,768]{1,0:T(8,128)(2,1)}, f32[256,768]{1,0:T(8,128)}, bf16[256,768]{1,0:T(8,128)(2,1)}, f32[16,256]{1,0:T(8,128)S(1)}, f32[8,768]{1,0...) custom-call(s32[7]{0:T(128)S(1)} %stack.39.refs_0_, f32[256,768]{1,0:T(8,128)S(1)} %copy-done.18, ...), custom_call_target="tpu_custom_call" | custom-call | flops 120795955200 | bytes 943718400 | tf_op jit(solution)/shard_map/branch_back/pallas_call | solution.py:58
  56.0 2.6 %combine.14 = (bf16[768,768]{1,0:T(8,128)(2,1)}, f32[8,128]{1,0:T(8,128)S(1)}) custom-call(bf16[1536,768]{1,0:T(8,128)(2,1)} %get-tuple-element.171.refs_0_, bf16[1536,768]{1,0:T(8,128)(2,1)} %collective-permute-done.5.refs_1_, f32[8,128]{1,0:T(8,128)S(1)} %get-tuple-element.173.refs_2_), custom_call_target="tpu_custom_call" | custom-call | flops 4300000256 | bytes 104857600 | tf_op jit(solution)/shard_map/combine/pallas_call | solution.py:58
  59.5 12.8 %attend_back.1 = (bf16[3,256,256]{2,1,0:T(8,128)(2,1)S(1)}, bf16[3,1024,256]{2,1,0:T(8,128)(2,1)S(1)}, bf16[3,1024,256]{2,1,0:T(8,128)(2,1)S(1)}, f32[8,128]{1,0:T(8,128)S(1)}) custom-call(bf16[256,768]{1,0:T(8,128)(2,1)} %get-tuple-element.165.refs_0_, bf16[3,1024,256]{2,1,0:T(8,128)(2,1)} %get-tuple-element.166.refs_1_, ...), custom_call_target="tpu_custom_call" | custom-call | flops 5000000000 | bytes 104857600 | tf_op jit(solution)/shard_map/attend_back/pallas_call | solution.py:58
  76.1 6.6 %weights.1 = (bf16[1568,768]{1,0:T(8,128)(2,1)}, bf16[1568,768]{1,0:T(8,128)(2,1)}, f32[8,128]{1,0:T(8,128)S(1)}) custom-call(s32[7]{0:T(128)S(1)} %stack.39.refs_0_, bf16[768,768]{1,0:T(8,128)(2,1)S(1)} %copy-done.15, f32[8,768]{1,0:T(8,128)S(1)} %get-tuple-element.183.refs_2_, f32[8,768]{1,0:T(8,128)S(1)} %get-tuple-element.184.refs_3_, ...), custom_call_target="tpu_custom_call" | custom-call | flops 271790899200 | bytes 943718400 | tf_op jit(solution)/shard_map/weights/pallas_call | solution.py:58
  89.5 3.5 %token_parts.1 = (f32[256,768]{1,0:T(8,128)S(1)}, bf16[512,768]{1,0:T(8,128)(2,1)S(1)}, bf16[256,768]{1,0:T(8,128)(2,1)S(1)}, f32[8,128]{1,0:T(8,128)S(1)}) custom-call(s32[7]{0:T(128)S(1)} %stack.39.refs_0_, bf16[768,768]{1,0:T(8,128)(2,1)S(1)} %copy-done.5, bf16[768,768]{1,0:T(8,128)(2,1)S(1)} %copy-done.6, bf16[768,768]{1,0:T(8,128)(2,1)S(1)} %copy-done.7, ...), custom_call_target="tpu_custom_call" | custom-call | flops 271790899200 | bytes 943718400 | tf_op jit(solution)/shard_map/token_parts/pallas_call | solution.py:58
  99.9 2.7 %collective-permute-start.12 = (bf16[96,768]{1,0:T(8,128)(2,1)S(1)}, bf16[96,768]{1,0:T(8,128)(2,1)S(1)}, u32[]{:S(2)}, u32[]{:S(2)}) collective-permute-start(bf16[96,768]{1,0:T(8,128)(2,1)S(1)} %get-tuple-element.197), channel_id=1, source_target_pairs={{0,16},{1,17},{2,18},{3,19},{4,12},{5,13},{6,14},{7,15},{8,24},{9,... | collective-permute-start | bytes 442376 | tf_op jit(solution)/shard_map/ppermute | solution.py:711
  109.5 4.7 %collective-permute-start.17 = (bf16[96,768]{1,0:T(8,128)(2,1)S(1)}, bf16[96,768]{1,0:T(8,128)(2,1)S(1)}, u32[]{:S(2)}, u32[]{:S(2)}) collective-permute-start(bf16[96,768]{1,0:T(8,128)(2,1)S(1)} %get-tuple-element.207.refs_0_), channel_id=1, source_target_pairs={{0,16},{1,17},{2,18},{3,19},{4,12},{5,13},{6,14},{7,15},{8,24},{9,... | collective-permute-start | bytes 442376 | tf_op jit(solution)/shard_map/ppermute | solution.py:711
  115.3 7.6 %collective-permute-done.18.refs_5_ = bf16[96,768]{1,0:T(8,128)(2,1)S(1)} collective-permute-done((bf16[96,768]{1,0:T(8,128)(2,1)S(1)}, bf16[96,768]{1,0:T(8,128)(2,1)S(1)}, u32[]{:S(2)}, u32[]{:S(2)}) %collective-permute-start.18) | collective-permute-done | bytes 147488 | tf_op jit(solution)/shard_map/ppermute | solution.py:711
  124.3 3.7 %collective-permute-start.20 = (bf16[192,768]{1,0:T(8,128)(2,1)S(1)}, bf16[192,768]{1,0:T(8,128)(2,1)S(1)}, u32[]{:S(2)}, u32[]{:S(2)}) collective-permute-start(bf16[192,768]{1,0:T(8,128)(2,1)S(1)} %get-tuple-element.215.refs_0_), channel_id=1, source_target_pairs={{0,8},{1,9},{2,10},{3,11},{4,20},{5,21},{6,22},{7,23},{8,0},{9,1},... | collective-permute-start | bytes 884744 | tf_op jit(solution)/shard_map/ppermute | solution.py:711
  131.3 4.2 %collective-permute-done.21.refs_1_ = bf16[96,768]{1,0:T(8,128)(2,1)S(1)} collective-permute-done((bf16[96,768]{1,0:T(8,128)(2,1)S(1)}, bf16[96,768]{1,0:T(8,128)(2,1)S(1)}, u32[]{:S(2)}, u32[]{:S(2)}) %collective-permute-start.21) | collective-permute-done | bytes 147488 | tf_op jit(solution)/shard_map/ppermute | solution.py:711
  136.7 3.1 %collective-permute-done.19.refs_3_.refs_5_ = bf16[416,768]{1,0:T(8,128)(2,1)S(1)} collective-permute-done((bf16[416,768]{1,0:T(8,128)(2,1)S(1)}, bf16[416,768]{1,0:T(8,128)(2,1)S(1)}, u32[]{:S(2)}, u32[]{:S(2)}) %collective-permute-start.19) | collective-permute-done | bytes 639008 | tf_op jit(solution)/shard_map/ppermute | solution.py:711
  143.6 4.4 %collective-permute-done.23.refs_1_ = bf16[384,768]{1,0:T(8,128)(2,1)S(1)} collective-permute-done((bf16[384,768]{1,0:T(8,128)(2,1)S(1)}, bf16[384,768]{1,0:T(8,128)(2,1)S(1)}, u32[]{:S(2)}, u32[]{:S(2)}) %collective-permute-start.23) | collective-permute-done | bytes 589856 | tf_op jit(solution)/shard_map/ppermute | solution.py:711
  153.3 12.7 %collective-permute-done.26.refs_1_ = bf16[384,768]{1,0:T(8,128)(2,1)S(1)} collective-permute-done((bf16[384,768]{1,0:T(8,128)(2,1)S(1)}, bf16[384,768]{1,0:T(8,128)(2,1)S(1)}, u32[]{:S(2)}, u32[]{:S(2)}) %collective-permute-start.26) | collective-permute-done | bytes 589856 | tf_op jit(solution)/shard_map/ppermute | solution.py:711
  170.3 4.5 %collective-permute-done.27.refs_1_ = bf16[96,768]{1,0:T(8,128)(2,1)S(1)} collective-permute-done((bf16[96,768]{1,0:T(8,128)(2,1)S(1)}, bf16[96,768]{1,0:T(8,128)(2,1)S(1)}, u32[]{:S(2)}, u32[]{:S(2)}) %collective-permute-start.27) | collective-permute-done | bytes 147488 | tf_op jit(solution)/shard_map/ppermute | solution.py:711
  177.1 5.2 %collective-permute-done.33.refs_2_ = bf16[768,768]{1,0:T(8,128)(2,1)S(1)} collective-permute-done((bf16[768,768]{1,0:T(8,128)(2,1)S(1)}, bf16[768,768]{1,0:T(8,128)(2,1)S(1)}, u32[]{:S(2)}, u32[]{:S(2)}) %collective-permute-start.33) | collective-permute-done | bytes 1179680 | tf_op jit(solution)/shard_map/ppermute | solution.py:711
  182.3 4.4 %unpack_rows.1 = (f32[3072,768]{1,0:T(8,128)}, f32[8,128]{1,0:T(8,128)S(1)}) custom-call(s32[7]{0:T(128)S(1)} %stack.39.refs_0_, bf16[768,768]{1,0:T(8,128)(2,1)S(1)} %get-tuple-element.233.refs_1_, bf16[768,768]{1,0:T(8,128)(2,1)S(1)} %collective-permute-done.29.refs_2_, bf16[768,768]{1,0:T(8,128)(2,1)S(1)} %collective-permute-done.30.refs_3_, ...), custom_call_target="tpu_custom_call" | custom-call | flops 235929600 | bytes 1415577600 | tf_op jit(solution)/shard_map/unpack_rows/pallas_call | solution.py:58
  191.9 5.1 %unpack_cols.1 = (f32[768,3072]{1,0:T(8,128)}, f32[8,128]{1,0:T(8,128)S(1)}) custom-call(s32[7]{0:T(128)S(1)} %stack.39.refs_0_, bf16[768,768]{1,0:T(8,128)(2,1)S(1)} %get-tuple-element.238.refs_1_, bf16[768,768]{1,0:T(8,128)(2,1)S(1)} %collective-permute-done.33.refs_2_, bf16[768,768]{1,0:T(8,128)(2,1)S(1)} %collective-permute-done.34.refs_3_, ...), custom_call_target="tpu_custom_call" | custom-call | flops 235929600 | bytes 1415577600 | tf_op jit(solution)/shard_map/unpack_cols/pallas_call | solution.py:58
  197.1 6.8 %collective-permute-done.32.refs_2_ = bf16[384,768]{1,0:T(8,128)(2,1)} collective-permute-done((bf16[384,768]{1,0:T(8,128)(2,1)}, bf16[384,768]{1,0:T(8,128)(2,1)}, u32[]{:S(2)}, u32[]{:S(2)}) %collective-permute-start.32) | collective-permute-done | bytes 589856 | tf_op jit(solution)/shard_map/ppermute | solution.py:711
  206.0 3.5 %unpack_four.4 = (f32[768,768]{1,0:T(8,128)}, f32[768,768]{1,0:T(8,128)}, f32[768,768]{1,0:T(8,128)}, f32[768,768]{1,0:T(8,128)}, f32[8,128]{1,0:T(8,128)S(1)}) custom-call(s32[7]{0:T(128)S(1)} %stack.39.refs_0_, bf16[384,768]{1,0:T(8,128)(2,1)} %get-tuple-element.236.refs_1_, bf16[384,768]{1,0:T(8,128)(2,1)} %collective-permute-done.32.refs_2_, ...), custom_call_target="tpu_custom_call" | custom-call | flops 235929600 | bytes 1415577600 | tf_op jit(solution)/shard_map/unpack_four/pallas_call | solution.py:58
  209.6 2.6 %unpack_four.5 = (f32[768,768]{1,0:T(8,128)}, f32[768,768]{1,0:T(8,128)}, f32[768,768]{1,0:T(8,128)}, f32[768,768]{1,0:T(8,128)}, f32[8,128]{1,0:T(8,128)S(1)}) custom-call(s32[7]{0:T(128)S(1)} %stack.39.refs_0_, bf16[384,768]{1,0:T(8,128)(2,1)} %collective-permute-done.37.refs_1_, ...), custom_call_target="tpu_custom_call", output_to_operand_aliasing={{0}: (3, {}), {1}: (4, {}), {2}: (5, {}), {3}: (6, {})} | custom-call | flops 235929600 | bytes 1415577600 | tf_op jit(solution)/shard_map/unpack_four/pallas_call | solution.py:58
  (167 shorter events, 81.9 us)
Async XLA Ops:
  0.7 12.6 %collective-permute-start.1 = (bf16[256,768]{1,0:T(8,128)(2,1)}, bf16[256,768]{1,0:T(8,128)(2,1)S(1)}, u32[]{:S(2)}, u32[]{:S(2)}) collective-permute-start(bf16[256,768]{1,0:T(8,128)(2,1)} %bitcast.20), channel_id=1, source_target_pairs={{0,2},{1,3},{2,0},{3,1},{4,6},{5,7},{6,4},{7,5},{8,10},{9,11},{10,... | collective-permute-start | bytes 1179656 | tf_op jit(solution)/shard_map/ppermute | solution.py:582
  3.7 11.1 %collective-permute-start = (bf16[256,768]{1,0:T(8,128)(2,1)}, bf16[256,768]{1,0:T(8,128)(2,1)S(1)}, u32[]{:S(2)}, u32[]{:S(2)}) collective-permute-start(bf16[256,768]{1,0:T(8,128)(2,1)} %bitcast.21), channel_id=1, source_target_pairs={{0,1},{1,0},{2,3},{3,2},{4,5},{5,4},{6,7},{7,6},{8,9},{9,8},{10,11... | collective-permute-start | bytes 1179656 | tf_op jit(solution)/shard_map/ppermute | solution.py:582
  50.5 21.8 %collective-permute-start.6 = (bf16[768,768]{1,0:T(8,128)(2,1)S(1)}, bf16[768,768]{1,0:T(8,128)(2,1)S(1)}, u32[]{:S(2)}, u32[]{:S(2)}) collective-permute-start(bf16[768,768]{1,0:T(8,128)(2,1)S(1)} %get-tuple-element.178), channel_id=1, source_target_pairs={{0,1},{1,0},{2,3},{3,2},{4,6},{5,7},{6,4},{7,5},{8,9},{9,8},{10,11... | collective-permute-start | bytes 3538952 | tf_op jit(solution)/shard_map/ppermute | solution.py:711
  58.6 24.1 %collective-permute-start.8 = (bf16[768,768]{1,0:T(8,128)(2,1)}, bf16[768,768]{1,0:T(8,128)(2,1)}, u32[]{:S(2)}, u32[]{:S(2)}) collective-permute-start(bf16[768,768]{1,0:T(8,128)(2,1)} %get-tuple-element.181), channel_id=1, source_target_pairs={{0,1},{1,0},{2,3},{3,2},{4,6},{5,7},{6,4},{7,5},{8,9},{9,8},{10,11... | collective-permute-start | bytes 3538952 | tf_op jit(solution)/shard_map/ppermute | solution.py:711
  74.6 11.2 %collective-permute-start.7 = (bf16[384,768]{1,0:T(8,128)(2,1)}, bf16[384,768]{1,0:T(8,128)(2,1)}, u32[]{:S(2)}, u32[]{:S(2)}) collective-permute-start(bf16[384,768]{1,0:T(8,128)(2,1)} %get-tuple-element.180), channel_id=1, source_target_pairs={{0,2},{1,3},{2,0},{3,1},{4,5},{5,4},{6,7},{7,6},{8,10},{9,11},{10,... | collective-permute-start | bytes 1769480 | tf_op jit(solution)/shard_map/ppermute | solution.py:711
  85.7 16.8 %collective-permute-start.14 = (bf16[1568,768]{1,0:T(8,128)(2,1)}, bf16[1568,768]{1,0:T(8,128)(2,1)}, u32[]{:S(2)}, u32[]{:S(2)}) collective-permute-start(bf16[1568,768]{1,0:T(8,128)(2,1)} %get-tuple-element.200), channel_id=1, source_target_pairs={{0,4},{4,0},{8,12},{12,8},{16,20},{20,16},{24,28},{28,24},{1,5},{5... | collective-permute-start | bytes 7225352 | tf_op jit(solution)/shard_map/ppermute | solution.py:582
  98.2 16.1 %collective-permute-start.9 = (bf16[512,768]{1,0:T(8,128)(2,1)S(1)}, bf16[512,768]{1,0:T(8,128)(2,1)S(1)}, u32[]{:S(2)}, u32[]{:S(2)}) collective-permute-start(bf16[512,768]{1,0:T(8,128)(2,1)S(1)} %get-tuple-element.191), channel_id=1, source_target_pairs={{0,1},{1,0},{2,3},{3,2},{4,6},{5,7},{6,4},{7,5},{8,9},{9,8},{10,11... | collective-permute-start | bytes 2359304 | tf_op jit(solution)/shard_map/ppermute | solution.py:711
  104.5 23.5 %collective-permute-start.16 = (bf16[800,768]{1,0:T(8,128)(2,1)S(1)}, bf16[800,768]{1,0:T(8,128)(2,1)S(1)}, u32[]{:S(2)}, u32[]{:S(2)}) collective-permute-start(bf16[800,768]{1,0:T(8,128)(2,1)S(1)} %get-tuple-element.206.refs_3_), channel_id=1, source_target_pairs={{0,1},{1,0},{2,3},{3,2},{4,6},{5,7},{6,4},{7,5},{8,9},{9,8},{10,11... | collective-permute-start | bytes 3686408 | tf_op jit(solution)/shard_map/ppermute | solution.py:711
  109.5 14.7 %collective-permute-start.17 = (bf16[96,768]{1,0:T(8,128)(2,1)S(1)}, bf16[96,768]{1,0:T(8,128)(2,1)S(1)}, u32[]{:S(2)}, u32[]{:S(2)}) collective-permute-start(bf16[96,768]{1,0:T(8,128)(2,1)S(1)} %get-tuple-element.207.refs_0_), channel_id=1, source_target_pairs={{0,16},{1,17},{2,18},{3,19},{4,12},{5,13},{6,14},{7,15},{8,24},{9,... | collective-permute-start | bytes 442376 | tf_op jit(solution)/shard_map/ppermute | solution.py:711
  114.3 16.0 %collective-permute-start.15 = (bf16[256,768]{1,0:T(8,128)(2,1)S(1)}, bf16[256,768]{1,0:T(8,128)(2,1)S(1)}, u32[]{:S(2)}, u32[]{:S(2)}) collective-permute-start(bf16[256,768]{1,0:T(8,128)(2,1)S(1)} %get-tuple-element.205), channel_id=1, source_target_pairs={{0,2},{1,3},{2,0},{3,1},{4,5},{5,4},{6,7},{7,6},{8,10},{9,11},{10,... | collective-permute-start | bytes 1179656 | tf_op jit(solution)/shard_map/ppermute | solution.py:711
  124.1 11.4 %collective-permute-start.21 = (bf16[96,768]{1,0:T(8,128)(2,1)S(1)}, bf16[96,768]{1,0:T(8,128)(2,1)S(1)}, u32[]{:S(2)}, u32[]{:S(2)}) collective-permute-start(bf16[96,768]{1,0:T(8,128)(2,1)S(1)} %get-tuple-element.216.refs_0_), channel_id=1, source_target_pairs={{0,16},{1,17},{2,18},{3,19},{4,12},{5,13},{6,14},{7,15},{8,24},{9,... | collective-permute-start | bytes 442376 | tf_op jit(solution)/shard_map/ppermute | solution.py:711
  124.3 11.4 %collective-permute-start.20 = (bf16[192,768]{1,0:T(8,128)(2,1)S(1)}, bf16[192,768]{1,0:T(8,128)(2,1)S(1)}, u32[]{:S(2)}, u32[]{:S(2)}) collective-permute-start(bf16[192,768]{1,0:T(8,128)(2,1)S(1)} %get-tuple-element.215.refs_0_), channel_id=1, source_target_pairs={{0,8},{1,9},{2,10},{3,11},{4,20},{5,21},{6,22},{7,23},{8,0},{9,1},... | collective-permute-start | bytes 884744 | tf_op jit(solution)/shard_map/ppermute | solution.py:711
  135.7 12.3 %collective-permute-start.23 = (bf16[384,768]{1,0:T(8,128)(2,1)S(1)}, bf16[384,768]{1,0:T(8,128)(2,1)S(1)}, u32[]{:S(2)}, u32[]{:S(2)}) collective-permute-start(bf16[384,768]{1,0:T(8,128)(2,1)S(1)} %get-tuple-element.221.refs_0_), channel_id=1, source_target_pairs={{0,2},{1,3},{2,0},{3,1},{4,5},{5,4},{6,7},{7,6},{8,10},{9,11},{10,... | collective-permute-start | bytes 1769480 | tf_op jit(solution)/shard_map/ppermute | solution.py:711
  148.1 18.5 %collective-permute-start.29 = (bf16[768,768]{1,0:T(8,128)(2,1)S(1)}, bf16[768,768]{1,0:T(8,128)(2,1)S(1)}, u32[]{:S(2)}, u32[]{:S(2)}) collective-permute-start(bf16[768,768]{1,0:T(8,128)(2,1)S(1)} %get-tuple-element.233.refs_1_), channel_id=1, source_target_pairs={{0,1},{1,0},{2,3},{3,2},{4,6},{5,7},{6,4},{7,5},{8,9},{9,8},{10,11... | collective-permute-start | bytes 3538952 | tf_op jit(solution)/shard_map/ppermute | solution.py:711
  149.7 16.3 %collective-permute-start.26 = (bf16[384,768]{1,0:T(8,128)(2,1)S(1)}, bf16[384,768]{1,0:T(8,128)(2,1)S(1)}, u32[]{:S(2)}, u32[]{:S(2)}) collective-permute-start(bf16[384,768]{1,0:T(8,128)(2,1)S(1)} %get-tuple-element.227.refs_0_), channel_id=1, source_target_pairs={{0,2},{1,3},{2,0},{3,1},{4,5},{5,4},{6,7},{7,6},{8,10},{9,11},{10,... | collective-permute-start | bytes 1769480 | tf_op jit(solution)/shard_map/ppermute | solution.py:711
  151.9 15.1 %collective-permute-start.25 = (bf16[128,768]{1,0:T(8,128)(2,1)S(1)}, bf16[128,768]{1,0:T(8,128)(2,1)S(1)}, u32[]{:S(2)}, u32[]{:S(2)}) collective-permute-start(bf16[128,768]{1,0:T(8,128)(2,1)S(1)} %get-tuple-element.226.refs_6_), channel_id=1, source_target_pairs={{0,16},{1,17},{2,18},{3,19},{4,12},{5,13},{6,14},{7,15},{8,24},{9,... | collective-permute-start | bytes 589832 | tf_op jit(solution)/shard_map/ppermute | solution.py:711
  166.0 16.3 %collective-permute-start.33 = (bf16[768,768]{1,0:T(8,128)(2,1)S(1)}, bf16[768,768]{1,0:T(8,128)(2,1)S(1)}, u32[]{:S(2)}, u32[]{:S(2)}) collective-permute-start(bf16[768,768]{1,0:T(8,128)(2,1)S(1)} %get-tuple-element.238.refs_1_), channel_id=1, source_target_pairs={{0,1},{1,0},{2,3},{3,2},{4,6},{5,7},{6,4},{7,5},{8,9},{9,8},{10,11... | collective-permute-start | bytes 3538952 | tf_op jit(solution)/shard_map/ppermute | solution.py:711
  166.6 15.7 %collective-permute-start.30 = (bf16[768,768]{1,0:T(8,128)(2,1)S(1)}, bf16[768,768]{1,0:T(8,128)(2,1)S(1)}, u32[]{:S(2)}, u32[]{:S(2)}) collective-permute-start(bf16[768,768]{1,0:T(8,128)(2,1)S(1)} %get-tuple-element.233.refs_1_), channel_id=1, source_target_pairs={{0,4},{4,0},{8,12},{12,8},{16,20},{20,16},{24,28},{28,24},{1,5},{5... | collective-permute-start | bytes 3538952 | tf_op jit(solution)/shard_map/ppermute | solution.py:582
  166.6 15.7 %collective-permute-start.31 = (bf16[768,768]{1,0:T(8,128)(2,1)S(1)}, bf16[768,768]{1,0:T(8,128)(2,1)S(1)}, u32[]{:S(2)}, u32[]{:S(2)}) collective-permute-start(bf16[768,768]{1,0:T(8,128)(2,1)S(1)} %collective-permute-done.29.refs_2_), channel_id=1, source_target_pairs={{0,4},{4,0},{8,12},{12,8},{16,20},{20,16},{24,28},{28,24},{1,5},{5... | collective-permute-start | bytes 3538952 | tf_op jit(solution)/shard_map/ppermute | solution.py:582
  174.9 11.8 %collective-permute-start.28 = (bf16[192,768]{1,0:T(8,128)(2,1)S(1)}, bf16[192,768]{1,0:T(8,128)(2,1)S(1)}, u32[]{:S(2)}, u32[]{:S(2)}) collective-permute-start(bf16[192,768]{1,0:T(8,128)(2,1)S(1)} %get-tuple-element.232.refs_0_), channel_id=1, source_target_pairs={{0,8},{1,9},{2,10},{3,11},{4,20},{5,21},{6,22},{7,23},{8,0},{9,1},... | collective-permute-start | bytes 884744 | tf_op jit(solution)/shard_map/ppermute | solution.py:711
  177.1 14.8 %collective-permute-start.34 = (bf16[768,768]{1,0:T(8,128)(2,1)S(1)}, bf16[768,768]{1,0:T(8,128)(2,1)S(1)}, u32[]{:S(2)}, u32[]{:S(2)}) collective-permute-start(bf16[768,768]{1,0:T(8,128)(2,1)S(1)} %get-tuple-element.238.refs_1_), channel_id=1, source_target_pairs={{0,4},{4,0},{8,12},{12,8},{16,20},{20,16},{24,28},{28,24},{1,5},{5... | collective-permute-start | bytes 3538952 | tf_op jit(solution)/shard_map/ppermute | solution.py:582
  187.6 16.2 %collective-permute-start.32 = (bf16[384,768]{1,0:T(8,128)(2,1)}, bf16[384,768]{1,0:T(8,128)(2,1)}, u32[]{:S(2)}, u32[]{:S(2)}) collective-permute-start(bf16[384,768]{1,0:T(8,128)(2,1)} %get-tuple-element.236.refs_1_), channel_id=1, source_target_pairs={{0,2},{1,3},{2,0},{3,1},{4,5},{5,4},{6,7},{7,6},{8,10},{9,11},{10,... | collective-permute-start | bytes 1769480 | tf_op jit(solution)/shard_map/ppermute | solution.py:711
  187.6 16.3 %collective-permute-start.37 = (bf16[384,768]{1,0:T(8,128)(2,1)}, bf16[384,768]{1,0:T(8,128)(2,1)}, u32[]{:S(2)}, u32[]{:S(2)}) collective-permute-start(bf16[384,768]{1,0:T(8,128)(2,1)} %get-tuple-element.236.refs_1_), channel_id=1, source_target_pairs={{0,1},{1,0},{2,3},{3,2},{4,6},{5,7},{6,4},{7,5},{8,9},{9,8},{10,11... | collective-permute-start | bytes 1769480 | tf_op jit(solution)/shard_map/ppermute | solution.py:711
  191.9 12.5 %collective-permute-start.39 = (bf16[384,768]{1,0:T(8,128)(2,1)}, bf16[384,768]{1,0:T(8,128)(2,1)S(1)}, u32[]{:S(2)}, u32[]{:S(2)}) collective-permute-start(bf16[384,768]{1,0:T(8,128)(2,1)} %get-tuple-element.236.refs_1_), channel_id=1, source_target_pairs={{0,4},{4,0},{8,12},{12,8},{16,20},{20,16},{24,28},{28,24},{1,5},{5... | collective-permute-start | bytes 1769480 | tf_op jit(solution)/shard_map/ppermute | solution.py:582
  (37 other events, 301.2 us)
